TPU v7x, 32 devices: a whole 2x2x4 slice. The times are simulated.
32 devices in a mesh: fsdp: 4 (over x, core), ctx: 8 (over z, y).
Axes of the slice: x: 2, y: 2, z: 4, core: 2. Of those that a mesh axis runs over, the one named last changes fastest.
Arguments:
- layer_in: bfloat16 [8, 4, 128, 1024], P('ctx', 'fsdp'), may hold values from -6 to 6
- grad_out: bfloat16 [8, 4, 128, 1024], P('ctx', 'fsdp'), may hold values from -6 to 6
- pair_of_rank: int32 [8], replicated, may hold values from 0 to 7, each once
- ln1_gain: bfloat16 [1024], P(('fsdp', 'ctx')), may hold values from 0.5 to 1.5
- ln1_bias: bfloat16 [1024], P(('fsdp', 'ctx')), may hold values from -1.5 to 1.5
- ln2_gain: bfloat16 [1024], P(('fsdp', 'ctx')), may hold values from 0.5 to 1.5
- ln2_bias: bfloat16 [1024], P(('fsdp', 'ctx')), may hold values from -1.5 to 1.5
- w_qkv: bfloat16 [1024, 3072], P(('fsdp', 'ctx')), may hold values from -4 to 4
- b_qkv: bfloat16 [3072], P(('fsdp', 'ctx')), may hold values from -2.5 to 2.5
- w_out: bfloat16 [1024, 1024], P(('fsdp', 'ctx')), may hold values from -3 to 3
- b_out: bfloat16 [1024], P(('fsdp', 'ctx')), may hold values from -2.5 to 2.5
- w_up: bfloat16 [1024, 4096], P(('fsdp', 'ctx')), may hold values from -0.1875 to 0.1875
- b_up: bfloat16 [4096], P(('fsdp', 'ctx')), may hold values from -2.5 to 2.5
- w_down: bfloat16 [1024, 4096], P(('fsdp', 'ctx')), may hold values from -0.09375 to 0.09375
- b_down: bfloat16 [1024], P(('fsdp', 'ctx')), may hold values from -2.5 to 2.5
Outputs:
- layer_out: bfloat16 [8, 4, 128, 1024], P('ctx', 'fsdp')
- grad_x: bfloat16 [8, 4, 128, 1024], P('ctx', 'fsdp')
- grad_ln1_gain: float32 [1024], P(('fsdp', 'ctx'))
- grad_ln1_bias: float32 [1024], P(('fsdp', 'ctx'))
- grad_ln2_gain: float32 [1024], P(('fsdp', 'ctx'))
- grad_ln2_bias: float32 [1024], P(('fsdp', 'ctx'))
- grad_w_qkv: float32 [1024, 3072], P(('fsdp', 'ctx'))
- grad_b_qkv: float32 [3072], P(('fsdp', 'ctx'))
- grad_w_out: float32 [1024, 1024], P(('fsdp', 'ctx'))
- grad_b_out: float32 [1024], P(('fsdp', 'ctx'))
- grad_w_up: float32 [1024, 4096], P(('fsdp', 'ctx'))
- grad_b_up: float32 [4096], P(('fsdp', 'ctx'))
- grad_w_down: float32 [1024, 4096], P(('fsdp', 'ctx'))
- grad_b_down: float32 [1024], P(('fsdp', 'ctx'))
Inputs may be any that keep to these rules, and one draw needn't show every extreme that they name: `pair_of_rank`: a permutation: each slot holds a different block pair, so block pairs 0 to 7 each appear once.
All inputs are finite; a program needn't handle non-finite values.
Results may differ from a plain program's by a relative error of at most 0.011.
Values may be sent and summed in bfloat16 or wider, within the bound.
A program may use at most 512 MiB of HBM per device.

v0:
```python
import math

import jax
import jax.numpy as jnp
from jax import lax
from jax.sharding import PartitionSpec as P

HD = 64
ROT = 16


EPS = 1e-05
NEG = -1e30
ROOT_HALF = 0.7071067811865476
INV_ROOT_TAU = 0.3989422804014327


def norm_parts(xf, scale_weight, shift_bias):
    row_mean = jnp.mean(xf, axis=-1, keepdims=True)
    centred_input = xf - row_mean
    inverse_deviation = lax.rsqrt(
        jnp.mean(centred_input * centred_input, axis=-1, keepdims=True) + EPS
    )
    normalized_input = centred_input * inverse_deviation
    return (
        normalized_input * scale_weight.astype(jnp.float32) + shift_bias.astype(jnp.float32),
        normalized_input,
        inverse_deviation,
    )


def layer_norm_backward(norm_output_gradient, normalized_input, inverse_deviation, scale_weight):
    normalized_gradient = norm_output_gradient * scale_weight.astype(jnp.float32)
    return inverse_deviation * (
        normalized_gradient
        - jnp.mean(normalized_gradient, axis=-1, keepdims=True)
        - normalized_input
        * jnp.mean(normalized_gradient * normalized_input, axis=-1, keepdims=True)
    )


def gelu_value(u):
    return 0.5 * u * (1.0 + lax.erf(u * ROOT_HALF))


def gelu_slope(u):
    return 0.5 * (1.0 + lax.erf(u * ROOT_HALF)) + u * jnp.exp(-0.5 * u * u) * INV_ROOT_TAU


def rotate(field, place, sign):
    half = ROT // 2
    freqs = jnp.exp(jnp.arange(half).astype(jnp.float32) * (-2.0 * math.log(10000.0) / ROT))
    angle = place.astype(jnp.float32)[..., None] * freqs
    cosine = jnp.cos(angle)[..., None, :]
    sine = sign * jnp.sin(angle)[..., None, :]
    first = field[..., :half]
    second = field[..., half:ROT]
    return jnp.concatenate(
        [first * cosine - second * sine, second * cosine + first * sine, field[..., rot_end() :]],
        axis=-1,
    )


def rot_end():
    return ROT


def leading(field, letters):
    return "n" + letters if field.ndim == 5 else letters


def product(left, left_letters, right, right_letters, result):
    form = leading(left, left_letters) + "," + leading(right, right_letters) + "->" + result
    return jnp.einsum(form, left, right, preferred_element_type=jnp.float32)


def selectors(sel):
    return (sel[:, None, None, None, None], sel[:, None, None, None], sel[:, None])


def visibility(sel, qpa, qpb, kpa, kpb):
    chosen = sel[:, None]
    key_place = jnp.where(chosen, kpa, kpb)
    query_place = jnp.where(chosen, qpa, qpb)
    return (key_place[:, None, :] <= query_place[:, :, None])[:, None, None]


def online_update(state, qa, qb, ka, kb, va, vb, qpa, qpb, kpa, kpb, sel, with_first, scale):
    top_a, total_a, acc_a, top_b, total_b, acc_b = state
    sel5, sel4, sel2 = selectors(sel)
    query_two = jnp.where(sel5, qa, qb)
    key_two = jnp.where(sel5, ka, kb)
    value_two = jnp.where(sel5, va, vb)
    visible = visibility(sel, qpa, qpb, kpa, kpb)
    score = jnp.where(visible, product(query_two, "sqhd", key_two, "skhd", "nshqk") * scale, NEG)
    peak_a = jnp.max(jnp.where(sel5, score, NEG), axis=(0, 4))
    peak_b = jnp.max(jnp.where(sel5, NEG, score), axis=(0, 4))
    if with_first:
        score_one = product(qb, "sqhd", ka, "skhd", "nshqk") * scale
        peak_b = jnp.maximum(peak_b, jnp.max(score_one, axis=(0, 4)))
    new_a = jnp.maximum(top_a, peak_a)
    new_b = jnp.maximum(top_b, peak_b)
    lifted = jnp.where(sel5, new_a[..., None], new_b[..., None])
    weight = jnp.where(visible, jnp.exp(score - lifted), 0.0)
    mixed = product(weight.astype(jnp.bfloat16), "shqk", value_two, "skhd", "nshqd")
    mass = jnp.sum(weight, axis=4)
    add_total_a = jnp.sum(jnp.where(sel4, mass, 0.0), axis=0)
    add_total_b = jnp.sum(jnp.where(sel4, 0.0, mass), axis=0)
    add_acc_a = jnp.sum(jnp.where(sel5, mixed, 0.0), axis=0)
    add_acc_b = jnp.sum(jnp.where(sel5, 0.0, mixed), axis=0)
    if with_first:
        weight_one = jnp.exp(score_one - new_b[..., None])
        add_total_b = add_total_b + jnp.sum(weight_one, axis=(0, 4))
        add_acc_b = add_acc_b + product(weight_one.astype(jnp.bfloat16), "shqk", va, "skhd", "shqd")
    decay_a = jnp.exp(top_a - new_a)
    decay_b = jnp.exp(top_b - new_b)
    return (
        new_a,
        total_a * decay_a + add_total_a,
        acc_a * decay_a[..., None] + add_acc_a,
        new_b,
        total_b * decay_b + add_total_b,
        acc_b * decay_b[..., None] + add_acc_b,
    )


def pair_terms(
    qa,
    qb,
    ka,
    kb,
    va,
    vb,
    da,
    db,
    lsea,
    lseb,
    dela,
    delb,
    qpa,
    qpb,
    kpa,
    kpb,
    sel,
    with_first,
    scale,
):
    sel5, sel4, sel2 = selectors(sel)
    query_two = jnp.where(sel5, qa, qb)
    key_two = jnp.where(sel5, ka, kb)
    value_two = jnp.where(sel5, va, vb)
    dctx_two = jnp.where(sel5, da, db)
    lse_two = jnp.where(sel4, lsea, lseb)
    delta_two = jnp.where(sel4, dela, delb)
    visible = visibility(sel, qpa, qpb, kpa, kpb)
    score = jnp.where(visible, product(query_two, "sqhd", key_two, "skhd", "nshqk") * scale, NEG)
    prob = jnp.exp(score - lse_two[..., None])
    dprob = product(dctx_two, "sqhd", value_two, "skhd", "nshqk")
    dscore = (scale * prob * (dprob - delta_two[..., None])).astype(jnp.bfloat16)
    first_ds = None
    first_prob = None
    if with_first:
        score_one = product(qb, "sqhd", ka, "skhd", "nshqk") * scale
        prob_one = jnp.exp(score_one - lseb[..., None])
        dprob_one = product(db, "sqhd", va, "skhd", "nshqk")
        first_ds = (scale * prob_one * (dprob_one - delb[..., None])).astype(jnp.bfloat16)
        first_prob = prob_one.astype(jnp.bfloat16)
    return (first_ds, first_prob, dscore, prob.astype(jnp.bfloat16))


def query_grads(terms, ka, kb, sel):
    sel5, sel4, sel2 = selectors(sel)
    key_two = jnp.where(sel5, ka, kb)
    dq_two = product(terms[2], "shqk", key_two, "skhd", "nsqhd")
    dq_a = jnp.where(sel5, dq_two, 0.0)
    dq_b = jnp.where(sel5, 0.0, dq_two)
    if terms[0] is not None:
        dq_b = dq_b + product(terms[0], "shqk", ka, "skhd", "nsqhd")
    return (dq_a, dq_b)


def key_grads(terms, qa, qb, da, db, sel):
    sel5, sel4, sel2 = selectors(sel)
    query_two = jnp.where(sel5, qa, qb)
    dctx_two = jnp.where(sel5, da, db)
    dk_two = product(terms[2], "shqk", query_two, "sqhd", "nskhd")
    dv_two = product(terms[3], "shqk", dctx_two, "sqhd", "nskhd")
    dk_a = jnp.where(sel5, dk_two, 0.0)
    dk_b = jnp.where(sel5, 0.0, dk_two)
    dv_a = jnp.where(sel5, dv_two, 0.0)
    dv_b = jnp.where(sel5, 0.0, dv_two)
    if terms[0] is not None:
        dk_a = dk_a + product(terms[0], "shqk", qb, "sqhd", "nskhd")
        dv_a = dv_a + product(terms[1], "shqk", db, "sqhd", "nskhd")
    return (dk_a, dk_b, dv_a, dv_b)


def tdot(left, right):
    return lax.dot_general(
        left, right, (((0,), (0,)), ((), ())), preferred_element_type=jnp.float32
    )


def rdot(left, right):
    return lax.dot_general(
        left, right, (((1,), (1,)), ((), ())), preferred_element_type=jnp.float32
    )


def shards(
    layer_in,
    grad_out,
    pair_of_rank,
    ln1_gain,
    ln1_bias,
    ln2_gain,
    ln2_bias,
    w_qkv,
    b_qkv,
    w_out,
    b_out,
    w_up,
    b_up,
    w_down,
    b_down,
):
    f32 = jnp.float32
    bf = jnp.bfloat16
    nctx = lax.axis_size("ctx")
    mine = pair_of_rank[lax.axis_index("ctx")]
    seqs = layer_in.shape[1]
    width2 = layer_in.shape[2]
    dmodel = layer_in.shape[3]
    blk = width2 // 2
    rows = seqs * width2
    heads = dmodel // HD
    scale = 1.0 / math.sqrt(HD)
    offsets = jnp.arange(blk, dtype=jnp.int32)
    place_a = mine * blk + offsets
    place_b = (2 * nctx - 1 - mine) * blk + offsets
    places = jnp.concatenate([place_a, place_b])
    params = (
        ln1_gain,
        ln1_bias,
        ln2_gain,
        ln2_bias,
        w_qkv,
        b_qkv,
        w_out,
        b_out,
        w_up,
        b_up,
        w_down,
        b_down,
    )
    full = (
        lax.all_gather(params[0], ("fsdp", "ctx"), axis=0, tiled=True),
        lax.all_gather(params[1], ("fsdp", "ctx"), axis=0, tiled=True),
        lax.all_gather(params[2], ("fsdp", "ctx"), axis=0, tiled=True),
        lax.all_gather(params[3], ("fsdp", "ctx"), axis=0, tiled=True),
        lax.all_gather(params[4], ("fsdp", "ctx"), axis=0, tiled=True),
        lax.all_gather(params[5], ("fsdp", "ctx"), axis=0, tiled=True),
        lax.all_gather(params[6], ("fsdp", "ctx"), axis=0, tiled=True),
        lax.all_gather(params[7], ("fsdp", "ctx"), axis=0, tiled=True),
        lax.all_gather(params[8], ("fsdp", "ctx"), axis=0, tiled=True),
        lax.all_gather(params[9], ("fsdp", "ctx"), axis=0, tiled=True),
        lax.all_gather(params[10], ("fsdp", "ctx"), axis=0, tiled=True),
        lax.all_gather(params[11], ("fsdp", "ctx"), axis=0, tiled=True),
    )
    xf = layer_in.reshape(rows, dmodel).astype(f32)
    norm1, hat1, rstd1 = norm_parts(xf, full[0], full[1])
    norm2, hat2, rstd2 = norm_parts(xf, full[2], full[3])
    norm1 = norm1.astype(bf)
    norm2 = norm2.astype(bf)
    qkv = jnp.dot(norm1, full[4], preferred_element_type=f32) + full[5].astype(f32)
    query = rotate(qkv[:, :dmodel].reshape(seqs, width2, heads, HD), places, 1.0).astype(bf)
    key = rotate(qkv[:, dmodel : 2 * dmodel].reshape(seqs, width2, heads, HD), places, 1.0).astype(
        bf
    )
    value = qkv[:, 2 * dmodel :].reshape(seqs, width2, heads, HD).astype(bf)
    query_a = query[:, :blk]
    query_b = query[:, blk:]
    key_b = key[:, blk:]
    value_b = value[:, blk:]
    lone = jnp.zeros((1,), dtype=bool)
    empty_top = jnp.full((seqs, heads, blk), NEG, f32)
    empty_total = jnp.zeros((seqs, heads, blk), f32)
    empty_acc = jnp.zeros((seqs, heads, blk, HD), f32)
    state = (empty_top, empty_total, empty_acc, empty_top, empty_total, empty_acc)
    state = online_update(
        state,
        query_a,
        query_b,
        key_b[None],
        key_b[None],
        value_b[None],
        value_b[None],
        place_a,
        place_b,
        place_b[None],
        place_b[None],
        lone,
        False,
        scale,
    )

    def key_parts(kpiece, vpiece, first):
        count = kpiece.shape[0]
        pairs = lax.dynamic_slice_in_dim(pair_of_rank, first, count)
        keys = kpiece.reshape(count, seqs, width2, heads, HD)
        values = vpiece.reshape(count, seqs, width2, heads, HD)
        kplace_a = pairs[:, None] * blk + offsets[None, :]
        kplace_b = (2 * nctx - 1 - pairs)[:, None] * blk + offsets[None, :]
        return (
            keys[:, :, :blk],
            keys[:, :, blk:],
            values[:, :, :blk],
            values[:, :, blk:],
            kplace_a,
            kplace_b,
            pairs,
        )

    key_send = key.reshape(1, seqs, width2, dmodel)
    value_send = value.reshape(1, seqs, width2, dmodel)
    ka, kb, va, vb, kpa, kpb, pairs = key_parts(
        lax.all_gather(key_send, "ctx", axis=0, tiled=True),
        lax.all_gather(value_send, "ctx", axis=0, tiled=True),
        jnp.int32(0),
    )
    state = online_update(
        state,
        query_a,
        query_b,
        ka,
        kb,
        va,
        vb,
        place_a,
        place_b,
        kpa,
        kpb,
        pairs <= mine,
        True,
        scale,
    )
    top_a, total_a, acc_a, top_b, total_b, acc_b = state
    context4 = jnp.concatenate([acc_a / total_a[..., None], acc_b / total_b[..., None]], axis=2)
    lse = jnp.concatenate([top_a + jnp.log(total_a), top_b + jnp.log(total_b)], axis=2)
    context = context4.transpose(0, 2, 1, 3).reshape(rows, dmodel).astype(bf)
    attn = jnp.dot(context, full[6], preferred_element_type=f32) + full[7].astype(f32)
    pre = jnp.dot(norm2, full[8], preferred_element_type=f32) + full[9].astype(f32)
    hidden = gelu_value(pre).astype(bf)
    mlp = rdot(hidden, full[10]) + full[11].astype(f32)
    layer_out = (xf + attn + mlp).astype(bf).reshape(layer_in.shape)
    again = (
        lax.all_gather(params[0], ("fsdp", "ctx"), axis=0, tiled=True),
        lax.all_gather(params[1], ("fsdp", "ctx"), axis=0, tiled=True),
        lax.all_gather(params[2], ("fsdp", "ctx"), axis=0, tiled=True),
        lax.all_gather(params[3], ("fsdp", "ctx"), axis=0, tiled=True),
        lax.all_gather(params[4], ("fsdp", "ctx"), axis=0, tiled=True),
        lax.all_gather(params[5], ("fsdp", "ctx"), axis=0, tiled=True),
        lax.all_gather(params[6], ("fsdp", "ctx"), axis=0, tiled=True),
        lax.all_gather(params[7], ("fsdp", "ctx"), axis=0, tiled=True),
        lax.all_gather(params[8], ("fsdp", "ctx"), axis=0, tiled=True),
        lax.all_gather(params[9], ("fsdp", "ctx"), axis=0, tiled=True),
        lax.all_gather(params[10], ("fsdp", "ctx"), axis=0, tiled=True),
        lax.all_gather(params[11], ("fsdp", "ctx"), axis=0, tiled=True),
    )
    grad_b = grad_out.reshape(rows, dmodel)
    grad_f = grad_b.astype(f32)
    dhidden = jnp.dot(grad_b, again[10], preferred_element_type=f32)
    dpre = dhidden * gelu_slope(pre)
    dpre_b = dpre.astype(bf)
    dnorm2 = rdot(dpre_b, again[8])
    dcontext = rdot(grad_b, again[6]).astype(bf)
    dctx4 = dcontext.reshape(seqs, width2, heads, HD)
    delta = jnp.sum(
        dctx4.astype(f32) * context.reshape(seqs, width2, heads, HD).astype(f32), axis=-1
    ).transpose(0, 2, 1)
    dctx_a = dctx4[:, :blk]
    dctx_b = dctx4[:, blk:]
    lse_a = lse[..., :blk]
    lse_b = lse[..., blk:]
    delta_a = delta[..., :blk]
    delta_b = delta[..., blk:]
    own = pair_terms(
        query_b,
        query_b,
        key_b[None],
        key_b[None],
        value_b[None],
        value_b[None],
        dctx_b,
        dctx_b,
        lse_b,
        lse_b,
        delta_b,
        delta_b,
        place_b,
        place_b,
        place_b[None],
        place_b[None],
        lone,
        False,
        scale,
    )
    own_dq = query_grads(own, key_b[None], key_b[None], lone)[1][0]
    own_keys = key_grads(own, query_b, query_b, dctx_b, dctx_b, lone)
    gathered = (
        lax.all_gather(key_send, "ctx", axis=0, tiled=True),
        lax.all_gather(value_send, "ctx", axis=0, tiled=True),
    )
    groups = math.gcd(nctx, 8)
    per = nctx // groups

    def group_terms(args):
        kpiece, vpiece, first = args
        ka, kb, va, vb, kpa, kpb, pairs = key_parts(kpiece, vpiece, first)
        sel = pairs <= mine
        terms = pair_terms(
            query_a,
            query_b,
            ka,
            kb,
            va,
            vb,
            dctx_a,
            dctx_b,
            lse_a,
            lse_b,
            delta_a,
            delta_b,
            place_a,
            place_b,
            kpa,
            kpb,
            sel,
            True,
            scale,
        )
        dq_a, dq_b = query_grads(terms, ka, kb, sel)
        return (terms, jnp.sum(dq_a, axis=0), jnp.sum(dq_b, axis=0))

    grouped = lax.map(
        group_terms,
        (
            gathered[0].reshape(groups, per, seqs, width2, dmodel),
            gathered[1].reshape(groups, per, seqs, width2, dmodel),
            jnp.arange(groups, dtype=jnp.int32) * per,
        ),
    )
    terms_all = tuple((part.reshape((nctx,) + part.shape[2:]) for part in grouped[0]))
    dq_a = jnp.sum(grouped[1], axis=0)
    dq_b = jnp.sum(grouped[2], axis=0)
    pairs = pair_of_rank
    sliced = tuple(
        (lax.slice_in_dim(part, 0, 1 * lax.axis_size("ctx"), axis=0) for part in terms_all)
    )
    dk_a, dk_b, dv_a, dv_b = key_grads(sliced, query_a, query_b, dctx_a, dctx_b, pairs <= mine)
    dkey = jnp.concatenate([dk_a, dk_b], axis=2).reshape(
        1 * lax.axis_size("ctx"), seqs, width2, dmodel
    )
    dval = jnp.concatenate([dv_a, dv_b], axis=2).reshape(
        1 * lax.axis_size("ctx"), seqs, width2, dmodel
    )
    kv_grad = lax.psum_scatter(
        jnp.concatenate([dkey, dval], axis=-1), "ctx", scatter_dimension=0, tiled=True
    )
    dkey = kv_grad[0, :, :, :dmodel].reshape(seqs, width2, heads, HD)
    dval = kv_grad[0, :, :, dmodel:].reshape(seqs, width2, heads, HD)
    zero_half = jnp.zeros((seqs, blk, heads, HD), f32)
    dquery = jnp.concatenate([dq_a, dq_b + own_dq], axis=1)
    dkey = dkey + jnp.concatenate([zero_half, own_keys[1][0]], axis=1)
    dval = dval + jnp.concatenate([zero_half, own_keys[3][0]], axis=1)
    dqkv = jnp.concatenate(
        [
            rotate(dquery, places, -1.0).reshape(rows, dmodel),
            rotate(dkey, places, -1.0).reshape(rows, dmodel),
            dval.reshape(rows, dmodel),
        ],
        axis=1,
    )
    dqkv_b = dqkv.astype(bf)
    dnorm1 = rdot(dqkv_b, again[4])
    grad_x = (
        (
            grad_f
            + layer_norm_backward(dnorm1, hat1, rstd1, again[0])
            + layer_norm_backward(dnorm2, hat2, rstd2, again[2])
        )
        .astype(bf)
        .reshape(layer_in.shape)
    )
    vectors = (
        lax.psum_scatter(
            jnp.sum(dnorm1 * hat1, axis=0), ("fsdp", "ctx"), scatter_dimension=0, tiled=True
        ),
        lax.psum_scatter(jnp.sum(dnorm1, axis=0), ("fsdp", "ctx"), scatter_dimension=0, tiled=True),
        lax.psum_scatter(
            jnp.sum(dnorm2 * hat2, axis=0), ("fsdp", "ctx"), scatter_dimension=0, tiled=True
        ),
        lax.psum_scatter(jnp.sum(dnorm2, axis=0), ("fsdp", "ctx"), scatter_dimension=0, tiled=True),
        lax.psum_scatter(jnp.sum(dqkv, axis=0), ("fsdp", "ctx"), scatter_dimension=0, tiled=True),
        lax.psum_scatter(jnp.sum(grad_f, axis=0), ("fsdp", "ctx"), scatter_dimension=0, tiled=True),
        lax.psum_scatter(jnp.sum(dpre, axis=0), ("fsdp", "ctx"), scatter_dimension=0, tiled=True),
    )
    weights = (
        lax.psum_scatter(tdot(norm1, dqkv_b), ("fsdp", "ctx"), scatter_dimension=0, tiled=True),
        lax.psum_scatter(tdot(context, grad_b), ("fsdp", "ctx"), scatter_dimension=0, tiled=True),
        lax.psum_scatter(tdot(norm2, dpre_b), ("fsdp", "ctx"), scatter_dimension=0, tiled=True),
        lax.psum_scatter(tdot(grad_b, hidden), ("fsdp", "ctx"), scatter_dimension=0, tiled=True),
    )
    return (
        layer_out,
        grad_x,
        vectors[0],
        vectors[1],
        vectors[2],
        vectors[3],
        weights[0],
        vectors[4],
        weights[1],
        vectors[5],
        weights[2],
        vectors[6],
        weights[3],
        vectors[5],
    )


def solution(mesh):
    return jax.shard_map(
        shards,
        mesh=mesh,
        in_specs=(
            P("ctx", "fsdp", None, None),
            P("ctx", "fsdp", None, None),
            P(),
            P(("fsdp", "ctx")),
            P(("fsdp", "ctx")),
            P(("fsdp", "ctx")),
            P(("fsdp", "ctx")),
            P(("fsdp", "ctx"), None),
            P(("fsdp", "ctx")),
            P(("fsdp", "ctx"), None),
            P(("fsdp", "ctx")),
            P(("fsdp", "ctx"), None),
            P(("fsdp", "ctx")),
            P(("fsdp", "ctx"), None),
            P(("fsdp", "ctx")),
        ),
        out_specs=(
            P("ctx", "fsdp", None, None),
            P("ctx", "fsdp", None, None),
            P(("fsdp", "ctx")),
            P(("fsdp", "ctx")),
            P(("fsdp", "ctx")),
            P(("fsdp", "ctx")),
            P(("fsdp", "ctx"), None),
            P(("fsdp", "ctx")),
            P(("fsdp", "ctx"), None),
            P(("fsdp", "ctx")),
            P(("fsdp", "ctx"), None),
            P(("fsdp", "ctx")),
            P(("fsdp", "ctx"), None),
            P(("fsdp", "ctx")),
        ),
        check_vma=False,
    )
```

profile of v0, /device:TPU:0, one launch (start us, length us, event | category | flops | bytes accessed | tf_op | source)
XLA Modules:
  0.0 1740.0 jit_solution(14961500150228062075)
XLA Ops:
  14.6 42.8 %all-reduce.17 = (bf16[1024]{0:T(1024)(128)(2,1)}, bf16[1024]{0:T(1024)(128)(2,1)}, bf16[1024]{0:T(1024)(128)(2,1)}, bf16[3072]{0:T(1024)(128)(2,1)S(1)}, bf16[1...) all-reduce(bf16[1024]{0:T(1024)(128)(2,1)S(1)} %dynamic-update-slic, ...), channel_id=1, replica_groups=mesh['fsdp'=4,'ctx'=8] {'fsdp','ctx'}, use_global_device_ids=true, to_apply=%add.8 | all-reduce | flops 9216 | bytes 36864
  62.4 20.8 %all-gather.9.cloned.1.call-done = bf16[1024,3072]{1,0:T(8,128)(2,1)} async-done(((bf16[32,3072]{1,0:T(8,128)(2,1)}), bf16[1024,3072]{1,0:T(8,128)(2,1)}) %all-gather.9.cloned.1.call-update) | async-done | bytes 6291472 | tf_op jit(solution)/shard_map/all_gather | solution.py:261
  83.3 4.0 convolution_add_fusion.2
  90.0 1.6 maximum_convert_fusion
  94.6 46.5 %all-gather.13.cloned.1.call-done = bf16[1024,1024]{1,0:T(8,128)(2,1)} async-done(((bf16[32,1024]{1,0:T(8,128)(2,1)}), bf16[1024,1024]{1,0:T(8,128)(2,1)}) %all-gather.13.cloned.1.call-update) | async-done | bytes 2097168 | tf_op jit(solution)/shard_map/all_gather | solution.py:263
  141.1 2.4 convolution_convert_fusion
  149.4 42.4 %all-gather.11.cloned.1.call-done = bf16[8,1,128,1024]{3,2,1,0:T(8,128)(2,1)} async-done(((bf16[1,1,128,1024]{3,2,1,0:T(8,128)(2,1)}), bf16[8,1,128,1024]{3,2,1,0:T(8,128)(2,1)}) %all-gather.11.cloned.1.call-update) | async-done | bytes 2097168 | tf_op jit(solution)/shard_map/all_gather | solution.py:327
  191.8 3.0 copy.214
  194.8 2.9 fusion.199
  197.7 3.1 copy.291
  200.8 4.0 copy.292
  204.8 37.2 %all-gather.19.cloned.1.call-done = bf16[1024,1024]{1,0:T(8,128)(2,1)} async-done(((bf16[128,1024]{1,0:T(8,128)(2,1)}), bf16[1024,1024]{1,0:T(8,128)(2,1)}) %all-gather.19.cloned.1.call-update) | async-done | bytes 2097168 | tf_op jit(solution)/shard_map/all_gather | solution.py:328
  242.0 6.8 reshape.1327
  248.8 3.1 fusion.198
  253.5 2.3 fusion.58
  255.9 2.1 select_reduce_fusion.3
  258.0 1.5 fusion.41
  260.9 2.2 select_reduce_fusion.1
  263.1 1.6 fusion.95
  266.2 115.7 %while.22 = (s32[]{:T(128)}, bf16[8,1,1,16,64,64]{4,5,3,2,1,0:T(8,128)(2,1)}, bf16[8,1,1,16,64,64]{4,5,3,2,1,0:T(8,128)(2,1)}, bf16[8,1,1,16,64,64]{5,4,3,2,1,0:...) while((s32[]{:T(128)}, ...), condition=%wide.region_15.16_spmd.clone.clone, body=%wide.region_14.15_spmd.clone.clone.sunk | while | flops 51845504 | bytes 11329422 | solution.py:445
  381.8 2.7 fusion.45
  384.5 2.1 bitcast_add_fusion.1
  387.5 2.0 fusion.39
  389.5 3.8 bitcast_add_fusion
  393.2 3.1 pad_maximum_fusion.1
  396.3 1.3 pad_maximum_fusion.2
  398.5 3.8 pad_maximum_fusion
  403.7 2.8 fusion.152
  406.8 3.5 reduce_sum.267
  410.3 2.8 reduce_sum.265
  416.3 132.2 %reduce-scatter.8.cloned.1.call-done = f32[1,1,128,2048]{2,3,1,0:T(8,128)} async-done(((f32[8,1,128,2048]{2,3,1,0:T(8,128)}), f32[1,1,128,2048]{2,3,1,0:T(8,128)}) %reduce-scatter.8.cloned.1.call-update) | async-done | bytes 1048592 | tf_op jit(solution)/shard_map/reduce_scatter | solution.py:467
  551.2 6.4 fusion.181
  558.4 67.7 %all-gather.1 = bf16[32,1,128]{2,1,0:T(2,128)(2,1)S(1)} all-gather(bf16[1,1,128]{2,1,0:T(2,128)(2,1)S(1)} %bitcast.558), channel_id=1, replica_groups=mesh['fsdp'=4,'ctx'=8] {'fsdp','ctx'}, dimensions={0}, use_global_device_ids=true | all-gather | bytes 8448 | tf_op jit(solution)/shard_map/all_gather | solution.py:266
  626.1 1.5 all-gather.15.cloned.1.call-done
  627.6 4.7 convolution_add_fusion.1
  632.4 74.0 %all-gather.17.cloned.1.call-done = bf16[1024,4096]{1,0:T(8,128)(2,1)} async-done(((bf16[32,4096]{1,0:T(8,128)(2,1)}), bf16[1024,4096]{1,0:T(8,128)(2,1)}) %all-gather.17.cloned.1.call-update) | async-done | bytes 8388624 | tf_op jit(solution)/shard_map/all_gather | solution.py:267
  706.3 5.6 fusion.204
  712.9 8.2 fusion.139
  721.5 9.1 convolution_bitcast_fusion.1
  730.5 17.6 %copy.280 = f32[1024,4096]{1,0:T(8,128)} copy(f32[1024,4096]{0,1:T(8,128)} %convolution_bitcast_fusion.1) | data formatting | bytes 33554432
  748.8 6.5 convolution_add_fusion.5
  756.5 6.5 fusion.141
  763.6 2.5 fusion.134
  767.2 40.4 %all-reduce.16 = (f32[1024]{0:T(1024)S(1)}, f32[1024]{0:T(1024)S(1)}, f32[1024]{0:T(1024)S(1)}, f32[1024]{0:T(1024)S(1)}, f32[3072]{0:T(1024)S(1)}, /*index=5*/f32[1024]{0:T(1024)S(1)}, f32[4096]{0:T(1024)S(1)}) all-reduce(f32[1024]{0:T(1024)S(1)} %get-tuple-element.395, ...), channel_id=4, replica_groups=mesh['fsdp'=4,'ctx'=8] {'fsdp','ctx'}, use_global_device_ids=true, to_apply=%region_24.25.clone | all-reduce | flops 12288 | bytes 98304
  811.2 42.4 %reduce-scatter.12.cloned.1.call-done = f32[32,1024]{1,0:T(8,128)} async-done(((f32[1024,1024]{1,0:T(8,128)}), f32[32,1024]{1,0:T(8,128)}) %reduce-scatter.12.cloned.1.call-update) | async-done | bytes 131088 | tf_op jit(solution)/shard_map/reduce_scatter | solution.py:510
  853.6 158.8 %reduce-scatter.10.cloned.1.call-done = f32[32,3072]{1,0:T(8,128)} async-done(((f32[1024,3072]{1,0:T(8,128)}), f32[32,3072]{1,0:T(8,128)}) %reduce-scatter.10.cloned.1.call-update) | async-done | bytes 393232 | tf_op jit(solution)/shard_map/reduce_scatter | solution.py:509
  1012.4 359.9 %reduce-scatter.14.cloned.1.call-done = f32[32,4096]{1,0:T(8,128)} async-done(((f32[1024,4096]{1,0:T(8,128)}), f32[32,4096]{1,0:T(8,128)}) %reduce-scatter.14.cloned.1.call-update) | async-done | bytes 524304 | tf_op jit(solution)/shard_map/reduce_scatter | solution.py:511
  1372.3 360.2 %reduce-scatter.16.cloned.1.call-done = f32[32,4096]{1,0:T(8,128)} async-done(((f32[1024,4096]{1,0:T(8,128)}), f32[32,4096]{1,0:T(8,128)}) %reduce-scatter.16.cloned.1.call-update) | async-done | bytes 524304
  (394 shorter events, 124.2 us)
Async XLA Ops:
  7.2 76.1 %all-gather.9.cloned.1.call-start = ((), (), s32[]{:S(2)}) async-start(), calls=%async_computation.5 | async-start | bytes 6488064 | tf_op jit(solution)/shard_map/all_gather | solution.py:261
  7.9 133.2 %all-gather.13.cloned.1.call-start = ((), (), s32[]{:S(2)}) async-start(), calls=%async_computation.7 | async-start | bytes 2162688 | tf_op jit(solution)/shard_map/all_gather | solution.py:263
  8.7 183.1 %all-gather.11.cloned.1.call-start = ((), (), s32[]{:S(2)}) async-start(), calls=%async_computation.6 | async-start | bytes 2359296 | tf_op jit(solution)/shard_map/all_gather | solution.py:327
  90.0 3.6 copy-start.39
  90.0 51.1 %copy-start.10 = (bf16[1,1,128,1024]{3,2,1,0:T(8,128)(2,1)S(1)}, bf16[1,1,128,1024]{3,2,1,0:T(8,128)(2,1)}, u32[]{:S(2)}) copy-start(bf16[1,1,128,1024]{3,2,1,0:T(8,128)(2,1)} %param.18) | copy-start | bytes 786436
  91.6 56.7 %copy-start.15 = (bf16[1,128,16,64]{3,1,2,0:T(8,128)(2,1)}, bf16[1,128,16,64]{3,1,2,0:T(8,128)(2,1)S(1)}, u32[]{:S(2)}) copy-start(bf16[1,128,16,64]{3,1,2,0:T(8,128)(2,1)S(1)} %maximum_convert_fusion) | copy-start | bytes 786436
  92.7 149.3 %all-gather.19.cloned.1.call-start = ((), (), s32[]{:S(2)}) async-start(), calls=%async_computation.14 | async-start | bytes 2359296 | tf_op jit(solution)/shard_map/all_gather | solution.py:328
  93.5 455.0 %reduce-scatter.8.cloned.1.call-start = ((), (), s32[]{:S(2)}) async-start(), calls=%async_computation.10 | async-start | bytes 9437184 | tf_op jit(solution)/shard_map/reduce_scatter | solution.py:467
  94.3 53.9 %copy-start.33 = (pred[64,64]{0,1:T(8,128)(4,1)}, pred[64,64]{0,1:T(8,128)(4,1)S(1)}, u32[]{:S(2)}) copy-start(pred[64,64]{0,1:T(8,128)(4,1)S(1)} %broadcast_compare_fusion.2) | copy-start | bytes 12292
  143.5 2.4 copy-start.23
  146.2 105.7 %copy-start.2 = (bf16[1,128,16,64]{1,3,2,0:T(8,128)(2,1)}, bf16[1,128,16,64]{1,3,2,0:T(8,128)(2,1)S(1)}, u32[]{:S(2)}) copy-start(bf16[1,128,16,64]{1,3,2,0:T(8,128)(2,1)S(1)} %pad_maximum_fusion.5) | copy-start | bytes 786436
  251.9 1.6 copy-start.4
  253.5 2.3 copy-start.27
  253.5 2.3 copy-start.28
  263.1 1.7 copy-start.29
  277.6 3.1 copy-start.32
  292.1 3.1 copy-start.32
  306.5 3.1 copy-start.32
  321.0 3.1 copy-start.32
  335.4 3.1 copy-start.32
  349.8 3.1 copy-start.32
  364.3 3.1 copy-start.32
  378.7 3.1 copy-start.32
  381.8 2.7 copy-start.3
  381.8 2.7 copy-start.24
  384.5 2.2 copy-start.22
  384.5 2.2 copy-start.25
  384.5 2.2 copy-start.26
  396.3 2.2 copy-start.1
  402.3 225.3 %all-gather.15.cloned.1.call-start = ((), (), s32[]{:S(2)}) async-start(), calls=%async_computation.8 | async-start | bytes 8650752 | tf_op jit(solution)/shard_map/all_gather | solution.py:265
  402.9 303.4 %all-gather.17.cloned.1.call-start = ((), (), s32[]{:S(2)}) async-start(), calls=%async_computation.9 | async-start | bytes 8650752 | tf_op jit(solution)/shard_map/all_gather | solution.py:267
  403.6 449.9 %reduce-scatter.12.cloned.1.call-start = ((), (), s32[]{:S(2)}) async-start(), calls=%async_computation.12 | async-start | bytes 4325376 | tf_op jit(solution)/shard_map/reduce_scatter | solution.py:510
  406.5 605.8 %reduce-scatter.10.cloned.1.call-start = ((), (), s32[]{:S(2)}) async-start(), calls=%async_computation.11 | async-start | bytes 12976128 | tf_op jit(solution)/shard_map/reduce_scatter | solution.py:509
  410.2 2.8 copy-start.9
  410.3 2.8 copy-start.30
  413.1 2.8 copy-start.16
  416.1 133.6 %copy-start.21 = (f32[1,64,16,64]{1,3,2,0:T(8,128)S(1)}, f32[1,64,16,64]{1,3,2,0:T(8,128)}, u32[]{:S(2)}) copy-start(f32[1,64,16,64]{1,3,2,0:T(8,128)} %convolution_bitcast_fusion.3) | copy-start | bytes 786436
  550.3 7.4 copy-start.6
  557.7 814.6 %reduce-scatter.14.cloned.1.call-start = ((), (), s32[]{:S(2)}) async-start(), calls=%async_computation.13 | async-start | bytes 17301504 | tf_op jit(solution)/shard_map/reduce_scatter | solution.py:511
  721.2 1011.3 %reduce-scatter.16.cloned.1.call-start = ((), (), s32[]{:S(2)}) async-start(), calls=%async_computation.15 | async-start | bytes 17301504
  748.8 6.5 copy-start.5
  748.8 6.5 copy-start.19
  748.8 7.7 copy-start.14
  748.8 14.8 slice-start
  755.3 8.3 slice-start.1
  756.5 6.6 copy-start.7
  763.6 2.6 copy-start.12
  807.7 925.3 %copy-start.41 = (f32[32]{0:T(128)}, f32[32]{0:T(128)S(1)}, u32[]{:S(2)}) copy-start(f32[32]{0:T(128)S(1)} %dynamic-slice.5) | copy-start | bytes 388
  (14 other events, 15.1 us)
Sparse Core Ops, SparseCore 0:
  10.9 72.3 all-gather.8
  86.2 54.8 all-gather.12
  143.8 47.9 all-gather.10
  194.3 47.6 all-gather.18
  402.4 145.9 reduce-scatter.7
  551.3 76.2 all-gather.14
  630.6 75.6 all-gather.16
  709.2 144.3 reduce-scatter.11
  860.2 152.1 reduce-scatter.9
  1015.1 357.1 reduce-scatter.13
  1375.2 357.3 reduce-scatter.15
where the time goes:
time: 1750 us; the launch traced here: 1740 us
  waiting for transfers between devices  1280 us (73%)
  blocking collectives  151 us (9%)
  matrix products  130 us (7%)
  local copies, waits for them, and re-layouts  95.7 us (5%)
  loops' own time  36.9 us (2%)
  other arithmetic  30.6 us (2%)
    unnamed x12, waiting for transfers between devices  363 us
    reduce_scatter x1, waiting for transfers between devices, shards(): lax.psum_scatter(tdot(norm2, dpre_b), ('fsdp', 'ctx'), scatter_dimension=...  360 us
    reduce_scatter x1, waiting for transfers between devices, shards(): lax.psum_scatter(tdot(norm1, dqkv_b), ('fsdp', 'ctx'), scatter_dimension=...  159 us
    reduce_scatter x1, waiting for transfers between devices, shards(): lax.psum_scatter(jnp.concatenate([dkey, dval], axis=-1), 'ctx', scatter_d...  132 us
    unnamed x2, blocking collectives  83.2 us
    all_gather x1, waiting for transfers between devices, shards(): lax.all_gather(params[10], ('fsdp', 'ctx'), axis=0, tiled=True)  74 us
    dot_general x62, matrix products, product(): return jnp.einsum(form, left, right, preferred_element_type=jnp.float32)  70 us
    all_gather x1, blocking collectives, shards(): lax.all_gather(params[9], ('fsdp', 'ctx'), axis=0, tiled=True)  67.7 us
  transfers between devices with their start and end apart: 11, of which 11 were waited for; matrix products, arithmetic and copies ran while one was open for 7% of the time, Pallas kernels for 0%

commit v1 on v0

--- a/solution.py
+++ b/solution.py
@@ -529,9 +529,246 @@
     )
 
 
+def span(lead, cols):
+    return jnp.arange(lead, dtype=jnp.int32)[:, None] if cols else jnp.arange(lead, dtype=jnp.int32)
+
+
+def turn(field, cosine, sine_low, sine_high):
+    half = ROT // 2
+    down = jnp.concatenate([field[:, half:], field[:, :half]], axis=1)
+    up = jnp.concatenate([field[:, -half:], field[:, :-half]], axis=1)
+    return field * cosine + down * sine_low + up * sine_high
+
+
+def turn_tables(places, width):
+    half = ROT // 2
+    lane = jnp.arange(width, dtype=jnp.int32) % HD
+    freqs = jnp.exp((lane % half).astype(jnp.float32) * (-2.0 * math.log(10000.0) / ROT))
+    angle = places.astype(jnp.float32)[:, None] * freqs[None, :]
+    cosine = jnp.where(lane < ROT, jnp.cos(angle), 1.0)
+    sine = jnp.sin(angle)
+    sine_low = jnp.where(lane < half, -sine, 0.0)
+    sine_high = jnp.where((lane >= half) & (lane < ROT), sine, 0.0)
+    return cosine, sine_low, sine_high
+
+
+def headed(field, count):
+    return field.reshape(field.shape[0], count, HD).transpose(1, 0, 2)
+
+
+def joined(field):
+    return field.transpose(1, 0, 2).reshape(field.shape[1], -1)
+
+
+def bdot(form, left, right):
+    return jnp.einsum(form, left, right, preferred_element_type=jnp.float32)
+
+
+def head_shards(
+    layer_in,
+    grad_out,
+    pair_of_rank,
+    ln1_gain,
+    ln1_bias,
+    ln2_gain,
+    ln2_bias,
+    w_qkv,
+    b_qkv,
+    w_out,
+    b_out,
+    w_up,
+    b_up,
+    w_down,
+    b_down,
+):
+    f32 = jnp.float32
+    bf = jnp.bfloat16
+    both = ("fsdp", "ctx")
+    nctx = lax.axis_size("ctx")
+    nf = lax.axis_size("fsdp")
+    ndev = nctx * nf
+    c = lax.axis_index("ctx")
+    seqs, width2, dmodel = layer_in.shape[1:]
+    blk = width2 // 2
+    own_rows = seqs * width2
+    ff = w_up.shape[1]
+    hloc = dmodel // HD // nctx
+    qw = hloc * HD
+    fw = ff // nctx
+    piece = dmodel // ndev
+    scale = 1.0 / math.sqrt(HD)
+
+    x_all = lax.all_gather(layer_in.reshape(own_rows, dmodel), "ctx", axis=0, tiled=True)
+    vec = jnp.concatenate([ln1_gain, ln1_bias, ln2_gain, ln2_bias, b_out, b_down, b_qkv, b_up])
+    vec = lax.all_gather(vec[None], both, axis=0, tiled=True)
+    cuts = [piece] * 6 + [b_qkv.shape[0], b_up.shape[0]]
+    fulls = []
+    at = 0
+    for cut in cuts:
+        fulls.append(vec[:, at : at + cut].reshape(-1).astype(f32))
+        at += cut
+    gain1, bias1, gain2, bias2, bo, bd, bq, bu = fulls
+    bq_c = lax.dynamic_slice_in_dim(bq.reshape(3, nctx, qw), c, 1, axis=1).reshape(1, 3 * qw)
+    bu_c = lax.dynamic_slice_in_dim(bu, c * fw, fw).reshape(1, fw)
+
+    def columns(parts):
+        packed = jnp.concatenate([p.reshape(piece, nctx, -1) for p in parts], axis=-1)
+        packed = packed.transpose(1, 0, 2)
+        got = lax.all_to_all(packed, "ctx", split_axis=0, concat_axis=0, tiled=True)
+        return got.reshape(nctx * piece, -1)
+
+    wq = w_qkv.reshape(piece, 3, nctx, qw).transpose(0, 2, 1, 3)
+    cols = lax.all_gather(columns([wq, w_up, w_down]), "fsdp", axis=0, tiled=True)
+    wq_c = cols[:, : 3 * qw]
+    wu_c = cols[:, 3 * qw : 3 * qw + fw]
+    wd_c = cols[:, 3 * qw + fw :]
+    there = [((nf * cc + f) , f * nctx + cc) for f in range(nf) for cc in range(nctx)]
+    back = [(b, a) for a, b in there]
+    wo_c = lax.all_gather(lax.ppermute(w_out, both, there), "fsdp", axis=0, tiled=True)
+    g_own = grad_out.reshape(own_rows, dmodel)
+    g_all = lax.all_gather(g_own, "ctx", axis=0, tiled=True)
+
+    rows = x_all.shape[0]
+    offsets = jnp.arange(blk, dtype=jnp.int32)
+    slot_a = pair_of_rank[:, None] * blk + offsets[None, :]
+    slot_b = (2 * nctx - 1 - pair_of_rank)[:, None] * blk + offsets[None, :]
+    slots = jnp.concatenate([slot_a, slot_b], axis=1)[:, None, :]
+    places = jnp.broadcast_to(slots, (nctx, seqs, width2)).reshape(rows)
+    group = jnp.broadcast_to(span(seqs, False)[None, :, None], (nctx, seqs, width2)).reshape(rows)
+
+    def hat_of(xf):
+        row_mean = jnp.mean(xf, axis=-1, keepdims=True)
+        centred = xf - row_mean
+        rstd = lax.rsqrt(jnp.mean(centred * centred, axis=-1, keepdims=True) + EPS)
+        return centred * rstd, rstd
+
+    hat, _ = hat_of(x_all.astype(f32))
+    norm1 = (hat * gain1 + bias1).astype(bf)
+    norm2 = (hat * gain2 + bias2).astype(bf)
+    qkv = jnp.dot(norm1, wq_c, preferred_element_type=f32) + bq_c
+    cosine, sine_low, sine_high = turn_tables(places, qw)
+    query = headed(turn(qkv[:, :qw], cosine, sine_low, sine_high).astype(bf), hloc)
+    key = headed(turn(qkv[:, qw : 2 * qw], cosine, sine_low, sine_high).astype(bf), hloc)
+    value = headed(qkv[:, 2 * qw :].astype(bf), hloc)
+    visible = places[None, :] <= places[:, None]
+    if seqs > 1:
+        visible = visible & (group[None, :] == group[:, None])
+    score = jnp.where(visible[None], bdot("hqd,hkd->hqk", query, key) * scale, NEG)
+    top = jnp.max(score, axis=-1, keepdims=True)
+    weight = jnp.exp(score - top)
+    total = jnp.sum(weight, axis=-1, keepdims=True)
+    mixed = bdot("hqk,hkd->hqd", weight.astype(bf), value)
+    context = (mixed / total).astype(bf)
+    lse = top + jnp.log(total)
+    ctx_c = joined(context)
+
+    pre = jnp.dot(norm2, wu_c, preferred_element_type=f32) + bu_c
+    hidden = gelu_value(pre).astype(bf)
+    part = rdot(hidden, wd_c) + jnp.dot(ctx_c, wo_c, preferred_element_type=f32)
+    fwd = lax.psum_scatter(part.astype(bf), "ctx", scatter_dimension=0, tiled=True)
+    x_own = layer_in.reshape(own_rows, dmodel).astype(f32)
+    layer_out = (x_own + fwd.astype(f32) + (bo + bd)).astype(bf).reshape(layer_in.shape)
+
+    dhidden = jnp.dot(g_all, wd_c, preferred_element_type=f32)
+    dpre = dhidden * gelu_slope(pre)
+    dpre_b = dpre.astype(bf)
+    dnorm2 = rdot(dpre_b, wu_c)
+    dctx = headed(rdot(g_all, wo_c).astype(bf), hloc)
+    delta = jnp.sum(dctx.astype(f32) * context.astype(f32), axis=-1, keepdims=True)
+    prob = jnp.exp(score - lse)
+    dprob = bdot("hqd,hkd->hqk", dctx, value)
+    ds = (scale * prob * (dprob - delta)).astype(bf)
+    dquery = joined(bdot("hqk,hkd->hqd", ds, key))
+    dkey = joined(bdot("hqk,hqd->hkd", ds, query))
+    dvalue = joined(bdot("hqk,hqd->hkd", prob.astype(bf), dctx))
+    dqkv = jnp.concatenate(
+        [
+            turn(dquery, cosine, -sine_low, -sine_high),
+            turn(dkey, cosine, -sine_low, -sine_high),
+            dvalue,
+        ],
+        axis=1,
+    )
+    dqkv_b = dqkv.astype(bf)
+    dnorm1 = rdot(dqkv_b, wq_c)
+    gsum = (dnorm1 * gain1 + dnorm2 * gain2).astype(bf)
+    gsum = lax.psum_scatter(gsum, "ctx", scatter_dimension=0, tiled=True).astype(f32)
+    hat_own, rstd_own = hat_of(x_own)
+    g_ownf = g_own.astype(f32)
+    grad_x = (
+        g_ownf
+        + rstd_own
+        * (
+            gsum
+            - jnp.mean(gsum, axis=-1, keepdims=True)
+            - hat_own * jnp.mean(gsum * hat_own, axis=-1, keepdims=True)
+        )
+    ).astype(bf).reshape(layer_in.shape)
+
+    wide = jnp.concatenate([tdot(norm1, dqkv_b), tdot(norm2, dpre_b), tdot(g_all, hidden)], axis=1)
+    wide = lax.psum_scatter(wide.astype(bf), "fsdp", scatter_dimension=0, tiled=True)
+    wide = lax.all_to_all(
+        wide.reshape(nctx, piece, -1), "ctx", split_axis=0, concat_axis=0, tiled=True
+    )
+    wide = wide.transpose(1, 0, 2).astype(f32)
+    grad_qkv = (
+        wide[:, :, : 3 * qw].reshape(piece, nctx, 3, qw).transpose(0, 2, 1, 3).reshape(piece, -1)
+    )
+    grad_up = wide[:, :, 3 * qw : 3 * qw + fw].reshape(piece, ff)
+    grad_down = wide[:, :, 3 * qw + fw :].reshape(piece, ff)
+    rows_out = tdot(ctx_c, g_all)
+    rows_out = lax.psum_scatter(rows_out.astype(bf), "fsdp", scatter_dimension=0, tiled=True)
+    grad_wout = lax.ppermute(rows_out, both, back).astype(f32)
+
+    sum_q = jnp.zeros((3, nctx, qw), f32)
+    sum_q = lax.dynamic_update_slice_in_dim(
+        sum_q, jnp.sum(dqkv, axis=0).reshape(3, 1, qw), c, axis=1
+    ).reshape(ndev, -1)
+    sum_u = lax.dynamic_update_slice_in_dim(
+        jnp.zeros((ff,), f32), jnp.sum(dpre, axis=0), c * fw, axis=0
+    ).reshape(ndev, -1)
+    sums = [
+        jnp.sum(dnorm1 * hat, axis=0).reshape(ndev, -1),
+        jnp.sum(dnorm1, axis=0).reshape(ndev, -1),
+        jnp.sum(dnorm2 * hat, axis=0).reshape(ndev, -1),
+        jnp.sum(dnorm2, axis=0).reshape(ndev, -1),
+        jnp.sum(g_ownf, axis=0).reshape(ndev, -1),
+        sum_q,
+        sum_u,
+    ]
+    sums = lax.psum_scatter(
+        jnp.concatenate(sums, axis=1), both, scatter_dimension=0, tiled=True
+    ).reshape(-1)
+    ends = [piece * i for i in range(6)] + [5 * piece + b_qkv.shape[0], sums.shape[0]]
+    vs = [sums[a:b] for a, b in zip(ends[:-1], ends[1:])]
+    return (
+        layer_out,
+        grad_x,
+        vs[0],
+        vs[1],
+        vs[2],
+        vs[3],
+        grad_qkv,
+        vs[5],
+        grad_wout,
+        vs[4],
+        grad_up,
+        vs[6],
+        grad_down,
+        vs[4],
+    )
+
+
 def solution(mesh):
+    nctx = mesh.shape["ctx"]
+
+    def pick(layer_in, *rest):
+        heads = layer_in.shape[-1] // HD
+        whole = heads % nctx == 0
+        return (head_shards if whole else shards)(layer_in, *rest)
+
     return jax.shard_map(
-        shards,
+        pick,
         mesh=mesh,
         in_specs=(
             P("ctx", "fsdp", None, None),

time: 1750 us -> 403 us (0.23)
  waiting for transfers between devices: 1280 us -> 177 us
  matrix products: 130 us -> 40.2 us
  local copies, waits for them, and re-layouts: 95.7 us -> 15.3 us
  loops' own time: 36.9 us -> 0 us
  blocking collectives: 151 us -> 126 us
    reduce_scatter x4, waiting for transfers between devices: 693 us -> 133 us  [the longest x1 69.5 us: head_shards(): lax.psum_scatter(part.astype(bf), 'ctx', scatter_dimension=0, tiled=True)]
    unnamed x12 -> x7, waiting for transfers between devices: 363 us -> 1.46 us
    all_gather x6 -> x3, waiting for transfers between devices: 222 us -> 41.8 us  [the longest x1 21.9 us: head_shards(): lax.all_gather(columns([wq, w_up, w_down]), 'fsdp', axis=0, tiled=True)]
    dot_general x66 -> x10, matrix products: 85.4 us -> 21.8 us  [the longest x6 13.4 us: bdot(): return jnp.einsum(form, left, right, preferred_element_type=jnp.float32)]
    all_gather x1, blocking collectives: 67.7 us -> 6.52 us  [head_shards(): lax.all_gather(lax.ppermute(w_out, both, there), 'fsdp', axis=0, tiled=True)]
    another operation x1 -> x0, loops' own time: 36.9 us -> none  [shards(): lax.map(group_terms, (gathered[0].reshape(groups, per, seqs, width2, dmod...]
    unnamed x116 -> x63, local copies, waits for them, and re-layouts: 42 us -> 7.31 us
    all_to_all x0 -> x1, blocking collectives: none -> 34.4 us  [columns(): got = lax.all_to_all(packed, 'ctx', split_axis=0, concat_axis=0, tiled=True)]
  transfers between devices with their start and end apart: 11 -> 10, of which waited for: 11 -> 5; matrix products, arithmetic and copies ran while one was open for 7% -> 9% of each run, Pallas kernels for 0% -> 0%
where the time goes in v1:
time: 403 us
  waiting for transfers between devices  177 us (44%)
  blocking collectives  126 us (31%)
  matrix products  40.2 us (10%)
  other arithmetic  21.8 us (5%)
  local copies, waits for them, and re-layouts  15.3 us (4%)
  between operations  14.8 us (4%)
  starting transfers between devices  8 us (2%)
    unnamed x2, blocking collectives  84.9 us
    reduce_scatter x1, waiting for transfers between devices, head_shards(): lax.psum_scatter(part.astype(bf), 'ctx', scatter_dimension=0, tiled=True)  69.5 us
    reduce_scatter x1, waiting for transfers between devices, head_shards(): lax.psum_scatter(gsum, 'ctx', scatter_dimension=0, tiled=True).astype(f32)  44.1 us
    all_to_all x1, blocking collectives, columns(): got = lax.all_to_all(packed, 'ctx', split_axis=0, concat_axis=0, tiled=True)  34.4 us
    all_gather x1, waiting for transfers between devices, head_shards(): lax.all_gather(columns([wq, w_up, w_down]), 'fsdp', axis=0, tiled=True)  21.9 us
    all_gather x1, waiting for transfers between devices, head_shards(): g_all = lax.all_gather(g_own, 'ctx', axis=0, tiled=True)  20 us
    reduce_scatter x1, waiting for transfers between devices, head_shards(): lax.psum_scatter(wide.astype(bf), 'fsdp', scatter_dimension=0, tiled=True)  19.6 us
    dot_general x6, matrix products, bdot(): return jnp.einsum(form, left, right, preferred_element_type=jnp.float32)  13.4 us
  transfers between devices with their start and end apart: 10, of which 5 were waited for; matrix products, arithmetic and copies ran while one was open for 9% of the time, Pallas kernels for 0%

profile of v1, /device:TPU:0, one launch (start us, length us, event | category | flops | bytes accessed | tf_op | source)
XLA Modules:
  0.0 402.6 jit_solution(15293305253915522857)
XLA Ops:
  8.0 0.7 all-gather.11.cloned.1.call-update
  8.7 1.0 copy.79
  9.9 1.1 copy.78
  10.9 1.0 copy.77
  12.1 34.4 %all_to_all.10 = bf16[8,32,1408]{2,1,0:T(8,128)(2,1)} all-to-all(bf16[8,32,1408]{2,1,0:T(8,128)(2,1)S(1)} %copy.58), channel_id=1, replica_groups=mesh['fsdp'=4,'ctx'=8] {'ctx'}, dimensions={0} | all-to-all | bytes 1441792 | tf_op jit(solution)/shard_map/all_to_all | solution.py:617
  47.7 43.3 %all-reduce = bf16[13312]{0:T(1024)(128)(2,1)S(1)} all-reduce(bf16[13312]{0:T(1024)(128)(2,1)S(1)} %dynamic-update-slice), channel_id=3, replica_groups=mesh['fsdp'=4,'ctx'=8] {'fsdp','ctx'}, use_global_device_ids=true, to_apply=%add | all-reduce | flops 13312 | bytes 53248
  92.7 6.5 %all_gather.18 = bf16[128,1024]{1,0:T(8,128)(2,1)S(1)} all-gather(bf16[32,1024]{1,0:T(8,128)(2,1)S(1)} %collective-permute-done), channel_id=1, replica_groups=mesh['fsdp'=4,'ctx'=8] {'fsdp'}, dimensions={0}, use_global_device_ids=true | all-gather | bytes 327680 | tf_op jit(solution)/shard_map/all_gather | solution.py:627
  99.3 2.3 convert_reduce_fusion
  102.4 20.0 %all-gather.11.cloned.1.call-done = bf16[1,1,1024,1024]{3,2,1,0:T(8,128)(2,1)} async-done(((bf16[1,1,128,1024]{3,2,1,0:T(8,128)(2,1)}), bf16[1,1,1024,1024]{3,2,1,0:T(8,128)(2,1)}) %all-gather.11.cloned.1.call-update) | async-done | bytes 2097168 | tf_op jit(solution)/shard_map/all_gather | solution.py:629
  122.4 3.1 fusion.45
  125.5 2.2 fusion.14
  127.8 21.9 %all-gather.7.cloned.1.call-done = bf16[1024,1408]{1,0:T(8,128)(2,1)} async-done(((bf16[256,1408]{1,0:T(8,128)(2,1)}), bf16[1024,1408]{1,0:T(8,128)(2,1)}) %all-gather.7.cloned.1.call-update) | async-done | bytes 2883600 | tf_op jit(solution)/shard_map/all_gather | solution.py:621
  149.6 2.8 convolution_add_fusion
  152.7 2.8 fusion.87
  155.6 1.9 fusion.3
  157.5 2.0 fusion
  159.5 3.3 multiply_reduce_fusion
  162.8 2.5 fusion.18
  165.4 3.5 multiply_convert_fusion
  168.8 0.8 fusion.132
  169.8 1.4 fusion.131
  171.3 3.0 fusion.82
  174.3 1.0 convolution_convert_fusion.1
  175.9 0.9 copy-done.13
  176.8 1.5 multiply_convert_fusion.1
  178.3 1.9 fusion.130
  180.3 1.3 fusion.42
  181.6 1.6 convolution_convert_fusion
  183.1 1.9 pad_maximum_fusion
  185.1 1.1 fusion.104
  186.2 0.7 copy-done.6
  186.9 1.1 fusion.48
  188.1 2.7 fusion.65
  190.9 4.7 %fusion.121 = (f32[1024]{0:T(1024)S(1)}, f32[1024]{0:T(1024)S(1)}, bf16[1024,1024]{1,0:T(8,128)(2,1)}, f32[1024]{0:T(1024)S(1)}, f32[1024]{0:T(1024)S(1)}) fusion(f32[1024]{0:T(1024)S(1)} %add_rsqrt_fusion, f32[1024]{0:T(1024)S(1)} %broadcast_multiply_fusion, bf16[1,1,1024,1024]{3,2,1,0:T(8,128)(2,1)S(1)} %copy-done.3, f32[1024]{0:T(1024)S(1)} %reshape.325, ...), kind=kOutput, calls=%fused_computation.175 | convolution fusion | flops 1087369216 | bytes 10518528 | tf_op jit(solution)/shard_map/dot_general | solution.py:205
  195.7 2.9 fusion.54
  198.6 2.1 add_convert_fusion.1
  201.6 19.6 %reduce-scatter.9.cloned.1.call-done = bf16[256,1408]{0,1:T(8,128)(2,1)} async-done(((bf16[1024,1408]{0,1:T(8,128)(2,1)}), bf16[256,1408]{0,1:T(8,128)(2,1)}) %reduce-scatter.9.cloned.1.call-update) | async-done | bytes 720912 | tf_op jit(solution)/shard_map/reduce_scatter | solution.py:709
  221.2 2.3 copy.65
  223.6 5.6 %all-to-all-start.1 = ((bf16[8,32,1408]{2,1,0:T(8,128)(2,1)}), bf16[8,32,1408]{2,1,0:T(8,128)(2,1)S(1)}, u32[]{:S(2)}, u32[]{:S(2)}) async-start(bf16[8,32,1408]{2,1,0:T(8,128)(2,1)} %bitcast.42), calls=%async_computation.4 | async-start | bytes 1441792 | tf_op jit(solution)/shard_map/all_to_all | solution.py:710
  229.8 41.6 %all-reduce.1 = f32[32,384]{1,0:T(8,128)S(1)} all-reduce(f32[32,384]{1,0:T(8,128)S(1)} %concatenate.55), channel_id=7, replica_groups=mesh['fsdp'=4,'ctx'=8] {'fsdp','ctx'}, use_global_device_ids=true, to_apply=%region_18.19.clone | all-reduce | flops 12288 | bytes 98304
  272.6 1.5 collective-permute-start.1
  275.3 44.1 %reduce-scatter.7.cloned.1.call-done = bf16[128,1024]{1,0:T(8,128)(2,1)} async-done(((bf16[1024,1024]{1,0:T(8,128)(2,1)}), bf16[128,1024]{1,0:T(8,128)(2,1)}) %reduce-scatter.7.cloned.1.call-update) | async-done | bytes 262160 | tf_op jit(solution)/shard_map/reduce_scatter | solution.py:695
  319.4 1.2 convert_reduce_fusion.1
  320.6 69.5 %reduce-scatter.5.cloned.1.call-done = bf16[128,1024]{1,0:T(8,128)(2,1)} async-done(((bf16[1024,1024]{1,0:T(8,128)(2,1)}), bf16[128,1024]{1,0:T(8,128)(2,1)}) %reduce-scatter.5.cloned.1.call-update) | async-done | bytes 262160 | tf_op jit(solution)/shard_map/reduce_scatter | solution.py:668
  390.1 2.0 fusion.108
  392.7 0.8 copy.82
  393.5 0.8 copy.75
  394.4 0.8 copy.76
  (136 shorter events, 10.9 us)
Async XLA Ops:
  7.2 92.1 %all-gather.9.cloned.1.call-start = ((), (), s32[]{:S(2)}) async-start(), calls=%async_computation.11 | async-start | bytes 2359296 | tf_op jit(solution)/shard_map/all_gather | solution.py:601
  7.9 114.5 %all-gather.11.cloned.1.call-start = ((), (), s32[]{:S(2)}) async-start(), calls=%async_computation.12 | async-start | bytes 2359296 | tf_op jit(solution)/shard_map/all_gather | solution.py:629
  8.7 141.0 %all-gather.7.cloned.1.call-start = ((), (), s32[]{:S(2)}) async-start(), calls=%async_computation.6 | async-start | bytes 3604480 | tf_op jit(solution)/shard_map/all_gather | solution.py:621
  9.7 36.9 %copy-start.23 = (bf16[32,1024]{1,0:T(8,128)(2,1)S(1)}, bf16[32,1024]{1,0:T(8,128)(2,1)}, u32[]{:S(2)}) copy-start(bf16[32,1024]{1,0:T(8,128)(2,1)} %param.24) | copy-start | bytes 196612
  9.8 37.5 %copy-start.14 = (bf16[32]{0:T(256)(128)(2,1)S(1)}, bf16[32]{0:T(256)(128)(2,1)}, u32[]{:S(2)}) copy-start(bf16[32]{0:T(256)(128)(2,1)} %param.18) | copy-start | bytes 196
  9.8 37.5 %copy-start.15 = (bf16[32]{0:T(256)(128)(2,1)S(1)}, bf16[32]{0:T(256)(128)(2,1)}, u32[]{:S(2)}) copy-start(bf16[32]{0:T(256)(128)(2,1)} %param.19) | copy-start | bytes 196
  9.8 37.5 %copy-start.16 = (bf16[32]{0:T(256)(128)(2,1)S(1)}, bf16[32]{0:T(256)(128)(2,1)}, u32[]{:S(2)}) copy-start(bf16[32]{0:T(256)(128)(2,1)} %param.20) | copy-start | bytes 196
  9.8 37.5 %copy-start.17 = (bf16[32]{0:T(256)(128)(2,1)S(1)}, bf16[32]{0:T(256)(128)(2,1)}, u32[]{:S(2)}) copy-start(bf16[32]{0:T(256)(128)(2,1)} %param.21) | copy-start | bytes 196
  9.8 37.5 %copy-start.18 = (bf16[32]{0:T(256)(128)(2,1)S(1)}, bf16[32]{0:T(256)(128)(2,1)}, u32[]{:S(2)}) copy-start(bf16[32]{0:T(256)(128)(2,1)} %param.25) | copy-start | bytes 196
  9.8 37.5 %copy-start.19 = (bf16[32]{0:T(256)(128)(2,1)S(1)}, bf16[32]{0:T(256)(128)(2,1)}, u32[]{:S(2)}) copy-start(bf16[32]{0:T(256)(128)(2,1)} %param.29) | copy-start | bytes 196
  9.8 37.5 %copy-start.20 = (bf16[96]{0:T(256)(128)(2,1)S(1)}, bf16[96]{0:T(256)(128)(2,1)}, u32[]{:S(2)}) copy-start(bf16[96]{0:T(256)(128)(2,1)} %param.23) | copy-start | bytes 580
  9.8 37.5 %copy-start.21 = (bf16[128]{0:T(256)(128)(2,1)S(1)}, bf16[128]{0:T(256)(128)(2,1)}, u32[]{:S(2)}) copy-start(bf16[128]{0:T(256)(128)(2,1)} %param.27) | copy-start | bytes 772
  10.9 80.9 %copy-start.24 = (s32[8]{0:T(128)S(1)}, s32[8]{0:T(128)}, u32[]{:S(2)}) copy-start(s32[8]{0:T(128)} %param.17) | copy-start | bytes 100
  46.5 174.7 %reduce-scatter.9.cloned.1.call-start = ((), (), s32[]{:S(2)}) async-start(), calls=%async_computation.9 | async-start | bytes 3604480 | tf_op jit(solution)/shard_map/reduce_scatter | solution.py:709
  46.6 46.1 %collective-permute-start = (bf16[32,1024]{1,0:T(8,128)(2,1)S(1)}, bf16[32,1024]{1,0:T(8,128)(2,1)S(1)}, u32[]{:S(2)}, u32[]{:S(2)}) collective-permute-start(bf16[32,1024]{1,0:T(8,128)(2,1)S(1)} %copy-done.23), channel_id=1, source_target_pairs={{0,0},{4,1},{8,2},{12,3},{16,4},{20,5},{24,6},{28,7},{1,8},{5,9},{... | collective-permute-start | bytes 196616 | tf_op jit(solution)/shard_map/ppermute | solution.py:627
  99.3 2.5 copy-start.1
  157.5 2.0 copy-start.12
  165.3 8.9 %copy-start.8 = (f32[2,1024,64]{1,2,0:T(8,128)}, f32[2,1024,64]{1,2,0:T(8,128)S(1)}, u32[]{:S(2)}) copy-start(f32[2,1024,64]{1,2,0:T(8,128)S(1)} %fusion.18) | copy-start | bytes 1572868
  171.2 3.1 copy-start.10
  174.3 1.6 copy-start.2
  174.3 2.4 copy-start.13
  176.7 1.6 copy-start
  178.3 2.0 copy-start.11
  180.3 2.9 copy-start.25
  185.0 87.5 %reduce-scatter.11.cloned.1.call-start = ((), (), s32[]{:S(2)}) async-start(), calls=%async_computation.10 | async-start | bytes 327680 | tf_op jit(solution)/shard_map/reduce_scatter | solution.py:720
  186.2 0.7 copy-start.6
  188.1 2.8 copy-start.3
  188.1 131.3 %reduce-scatter.7.cloned.1.call-start = ((), (), s32[]{:S(2)}) async-start(), calls=%async_computation.8 | async-start | bytes 2359296 | tf_op jit(solution)/shard_map/reduce_scatter | solution.py:695
  188.1 2.8 copy-start.26
  195.7 2.9 copy-start.7
  195.7 194.5 %reduce-scatter.5.cloned.1.call-start = ((), (), s32[]{:S(2)}) async-start(), calls=%async_computation.7 | async-start | bytes 2359296 | tf_op jit(solution)/shard_map/reduce_scatter | solution.py:668
  198.6 2.3 copy-start.5
  198.6 2.4 copy-start.4
  200.7 28.4 %copy-start.9 = (f32[2,1024,64]{1,2,0:T(8,128)S(1)}, f32[2,1024,64]{1,2,0:T(8,128)}, u32[]{:S(2)}) copy-start(f32[2,1024,64]{1,2,0:T(8,128)} %copy-done.8) | copy-start | bytes 1572868
  223.6 168.6 %all-to-all-start.1 = ((bf16[8,32,1408]{2,1,0:T(8,128)(2,1)}), bf16[8,32,1408]{2,1,0:T(8,128)(2,1)S(1)}, u32[]{:S(2)}, u32[]{:S(2)}) async-start(bf16[8,32,1408]{2,1,0:T(8,128)(2,1)} %bitcast.42), calls=%async_computation.4 | async-start | bytes 1441792 | tf_op jit(solution)/shard_map/all_to_all | solution.py:710
  272.0 123.2 %copy-start.22 = (f32[32]{0:T(128)}, f32[32]{0:T(128)S(1)}, u32[]{:S(2)}) copy-start(f32[32]{0:T(128)S(1)} %get-tuple-element.101) | copy-start | bytes 388
  272.6 2.1 collective-permute-start.1
Sparse Core Ops, SparseCore 0:
  10.1 61.9 all-gather.8
  74.2 48.1 all-gather.10
  124.0 25.6 all-gather.6
  185.2 36.0 reduce-scatter.8
  224.1 20.1 reduce-scatter.10
  247.7 71.6 reduce-scatter.6
  322.9 67.1 reduce-scatter.4

commit v2 on v1

--- a/solution.py
+++ b/solution.py
@@ -7,6 +7,7 @@
 
 HD = 64
 ROT = 16
+LANES = 128
 
 
 EPS = 1e-05
@@ -599,18 +600,6 @@
     scale = 1.0 / math.sqrt(HD)
 
     x_all = lax.all_gather(layer_in.reshape(own_rows, dmodel), "ctx", axis=0, tiled=True)
-    vec = jnp.concatenate([ln1_gain, ln1_bias, ln2_gain, ln2_bias, b_out, b_down, b_qkv, b_up])
-    vec = lax.all_gather(vec[None], both, axis=0, tiled=True)
-    cuts = [piece] * 6 + [b_qkv.shape[0], b_up.shape[0]]
-    fulls = []
-    at = 0
-    for cut in cuts:
-        fulls.append(vec[:, at : at + cut].reshape(-1).astype(f32))
-        at += cut
-    gain1, bias1, gain2, bias2, bo, bd, bq, bu = fulls
-    bq_c = lax.dynamic_slice_in_dim(bq.reshape(3, nctx, qw), c, 1, axis=1).reshape(1, 3 * qw)
-    bu_c = lax.dynamic_slice_in_dim(bu, c * fw, fw).reshape(1, fw)
-
     def columns(parts):
         packed = jnp.concatenate([p.reshape(piece, nctx, -1) for p in parts], axis=-1)
         packed = packed.transpose(1, 0, 2)
@@ -618,15 +607,30 @@
         return got.reshape(nctx * piece, -1)
 
     wq = w_qkv.reshape(piece, 3, nctx, qw).transpose(0, 2, 1, 3)
-    cols = lax.all_gather(columns([wq, w_up, w_down]), "fsdp", axis=0, tiled=True)
+    vec = jnp.concatenate([ln1_gain, ln1_bias, ln2_gain, ln2_bias, b_out, b_down, b_qkv, b_up])
+    vw = LANES * -(-vec.shape[0] // (piece * LANES))
+    vec_pad = jnp.pad(vec, (0, piece * vw - vec.shape[0])).reshape(piece, 1, vw)
+    vec_pad = jnp.broadcast_to(vec_pad, (piece, nctx, vw))
+    cols = lax.all_gather(columns([wq, w_up, w_down, vec_pad]), "fsdp", axis=0, tiled=True)
+    g_own = grad_out.reshape(own_rows, dmodel)
+    cols, g_send = lax.optimization_barrier((cols, g_own))
+    got = cols[:, 3 * qw + 2 * fw :].reshape(ndev, piece * vw)
+    cuts = [piece] * 6 + [b_qkv.shape[0], b_up.shape[0]]
+    fulls = []
+    at = 0
+    for cut in cuts:
+        fulls.append(got[:, at : at + cut].reshape(-1).astype(f32))
+        at += cut
+    gain1, bias1, gain2, bias2, bo, bd, bq, bu = fulls
+    bq_c = lax.dynamic_slice_in_dim(bq.reshape(3, nctx, qw), c, 1, axis=1).reshape(1, 3 * qw)
+    bu_c = lax.dynamic_slice_in_dim(bu, c * fw, fw).reshape(1, fw)
     wq_c = cols[:, : 3 * qw]
     wu_c = cols[:, 3 * qw : 3 * qw + fw]
-    wd_c = cols[:, 3 * qw + fw :]
+    wd_c = cols[:, 3 * qw + fw : 3 * qw + 2 * fw]
     there = [((nf * cc + f) , f * nctx + cc) for f in range(nf) for cc in range(nctx)]
     back = [(b, a) for a, b in there]
     wo_c = lax.all_gather(lax.ppermute(w_out, both, there), "fsdp", axis=0, tiled=True)
-    g_own = grad_out.reshape(own_rows, dmodel)
-    g_all = lax.all_gather(g_own, "ctx", axis=0, tiled=True)
+    g_all = lax.all_gather(g_send, "ctx", axis=0, tiled=True)
 
     rows = x_all.shape[0]
     offsets = jnp.arange(blk, dtype=jnp.int32)
@@ -665,9 +669,12 @@
     pre = jnp.dot(norm2, wu_c, preferred_element_type=f32) + bu_c
     hidden = gelu_value(pre).astype(bf)
     part = rdot(hidden, wd_c) + jnp.dot(ctx_c, wo_c, preferred_element_type=f32)
-    fwd = lax.psum_scatter(part.astype(bf), "ctx", scatter_dimension=0, tiled=True)
+    fwd = lax.all_to_all(
+        part.astype(bf).reshape(nctx, own_rows, dmodel), "ctx", split_axis=0, concat_axis=0, tiled=True
+    )
+    fwd = jnp.sum(fwd.astype(f32), axis=0)
     x_own = layer_in.reshape(own_rows, dmodel).astype(f32)
-    layer_out = (x_own + fwd.astype(f32) + (bo + bd)).astype(bf).reshape(layer_in.shape)
+    layer_out = (x_own + fwd + (bo + bd)).astype(bf).reshape(layer_in.shape)
 
     dhidden = jnp.dot(g_all, wd_c, preferred_element_type=f32)
     dpre = dhidden * gelu_slope(pre)
@@ -705,21 +712,6 @@
         )
     ).astype(bf).reshape(layer_in.shape)
 
-    wide = jnp.concatenate([tdot(norm1, dqkv_b), tdot(norm2, dpre_b), tdot(g_all, hidden)], axis=1)
-    wide = lax.psum_scatter(wide.astype(bf), "fsdp", scatter_dimension=0, tiled=True)
-    wide = lax.all_to_all(
-        wide.reshape(nctx, piece, -1), "ctx", split_axis=0, concat_axis=0, tiled=True
-    )
-    wide = wide.transpose(1, 0, 2).astype(f32)
-    grad_qkv = (
-        wide[:, :, : 3 * qw].reshape(piece, nctx, 3, qw).transpose(0, 2, 1, 3).reshape(piece, -1)
-    )
-    grad_up = wide[:, :, 3 * qw : 3 * qw + fw].reshape(piece, ff)
-    grad_down = wide[:, :, 3 * qw + fw :].reshape(piece, ff)
-    rows_out = tdot(ctx_c, g_all)
-    rows_out = lax.psum_scatter(rows_out.astype(bf), "fsdp", scatter_dimension=0, tiled=True)
-    grad_wout = lax.ppermute(rows_out, both, back).astype(f32)
-
     sum_q = jnp.zeros((3, nctx, qw), f32)
     sum_q = lax.dynamic_update_slice_in_dim(
         sum_q, jnp.sum(dqkv, axis=0).reshape(3, 1, qw), c, axis=1
@@ -736,9 +728,33 @@
         sum_q,
         sum_u,
     ]
-    sums = lax.psum_scatter(
-        jnp.concatenate(sums, axis=1), both, scatter_dimension=0, tiled=True
-    ).reshape(-1)
+    sums = jnp.concatenate(sums, axis=1)
+    sw = LANES * -(-sums.shape[1] // (piece * LANES))
+    sums_pad = jnp.pad(sums, ((0, 0), (0, piece * sw - sums.shape[1]))).reshape(ndev * piece, sw)
+    rows_out = tdot(ctx_c, g_all).astype(bf)
+    wide = jnp.concatenate(
+        [
+            tdot(norm1, dqkv_b).astype(bf),
+            tdot(norm2, dpre_b).astype(bf),
+            tdot(g_all, hidden).astype(bf),
+            sums_pad.astype(bf),
+            rows_out.reshape(ndev * piece, -1),
+        ],
+        axis=1,
+    )
+    wide = lax.psum_scatter(wide, "fsdp", scatter_dimension=0, tiled=True)
+    split = 3 * qw + 2 * fw + sw
+    grad_wout = lax.ppermute(wide[:, split:].reshape(piece, dmodel), both, back).astype(f32)
+    wide = lax.all_to_all(
+        wide[:, :split].reshape(nctx, piece, split), "ctx", split_axis=0, concat_axis=0, tiled=True
+    )
+    sums = jnp.sum(wide[:, :, split - sw :].astype(f32), axis=0).reshape(-1)[: sums.shape[1]]
+    wide = wide.transpose(1, 0, 2).astype(f32)
+    grad_qkv = (
+        wide[:, :, : 3 * qw].reshape(piece, nctx, 3, qw).transpose(0, 2, 1, 3).reshape(piece, -1)
+    )
+    grad_up = wide[:, :, 3 * qw : 3 * qw + fw].reshape(piece, ff)
+    grad_down = wide[:, :, 3 * qw + fw : 3 * qw + 2 * fw].reshape(piece, ff)
     ends = [piece * i for i in range(6)] + [5 * piece + b_qkv.shape[0], sums.shape[0]]
     vs = [sums[a:b] for a, b in zip(ends[:-1], ends[1:])]
     return (

time: 403 us -> 350 us (0.87); the launches traced: 403 us -> 345 us
  blocking collectives: 126 us -> 46.8 us
  local copies, waits for them, and re-layouts: 15.3 us -> 36.2 us
  matrix products: 40.2 us -> 55.2 us
  waiting for transfers between devices: 177 us -> 164 us
    reduce_scatter x3 -> x1, waiting for transfers between devices: 89.1 us -> 0.01 us  [head_shards(): wide = lax.psum_scatter(wide, 'fsdp', scatter_dimension=0, tiled=True)]
    unnamed x2 -> x0, blocking collectives: 84.9 us -> none
    all_to_all x1 -> x2, waiting for transfers between devices: 0.01 us -> 53.6 us  [the longest x1 53.6 us: head_shards(): lax.all_to_all(part.astype(bf).reshape(nctx, own_rows, dmodel), 'ctx', sp...]
    all_gather x2, waiting for transfers between devices: 41.8 us -> 56.7 us  [the longest x1 30.3 us: head_shards(): g_all = lax.all_gather(g_send, 'ctx', axis=0, tiled=True)]
    all_gather x1, blocking collectives: 6.52 us -> 13.3 us  [head_shards(): lax.all_gather(lax.ppermute(w_out, both, there), 'fsdp', axis=0, tiled=True)]
    dot_general x4, matrix products: 4.99 us -> 11.1 us  [tdot(): lax.dot_general(left, right, (((0,), (0,)), ((), ())), preferred_element_...]
    reshape x1 -> x5, local copies, waits for them, and re-layouts: 0.83 us -> 6.19 us  [the longest x2 3.56 us: head_shards(): rows_out.reshape(ndev * piece, -1)]
    concatenate x1, local copies, waits for them, and re-layouts: 0.1 us -> 5.44 us  [head_shards(): jnp.concatenate([ln1_gain, ln1_bias, ln2_gain, ln2_bias, b_out, b_down, b...]
  transfers between devices with their start and end apart: 10 -> 9, of which waited for: 5 -> 5; matrix products, arithmetic and copies ran while one was open for 9% -> 13% of each run, Pallas kernels for 0% -> 0%
where the time goes in v2:
time: 350 us; the launch traced here: 345 us
  waiting for transfers between devices  164 us (47%)
  matrix products  55.2 us (16%)
  blocking collectives  46.8 us (13%)
  local copies, waits for them, and re-layouts  36.2 us (10%)
  other arithmetic  19.4 us (6%)
  between operations  14.4 us (4%)
  starting transfers between devices  8.9 us (3%)
    all_to_all x1, waiting for transfers between devices, head_shards(): lax.all_to_all(part.astype(bf).reshape(nctx, own_rows, dmodel), 'ctx', sp...  53.6 us
    reduce_scatter x1, waiting for transfers between devices, head_shards(): lax.psum_scatter(gsum, 'ctx', scatter_dimension=0, tiled=True).astype(f32)  47 us
    all_to_all x1, blocking collectives, columns(): got = lax.all_to_all(packed, 'ctx', split_axis=0, concat_axis=0, tiled=True)  33.5 us
    all_gather x1, waiting for transfers between devices, head_shards(): g_all = lax.all_gather(g_send, 'ctx', axis=0, tiled=True)  30.3 us
    all_gather x1, waiting for transfers between devices, head_shards(): lax.all_gather(columns([wq, w_up, w_down, vec_pad]), 'fsdp', axis=0, tile...  26.4 us
    dot_general x6, matrix products, bdot(): return jnp.einsum(form, left, right, preferred_element_type=jnp.float32)  15.8 us
    dot_general x4, matrix products, rdot(): lax.dot_general(left, right, (((1,), (1,)), ((), ())), preferred_element_...  14.6 us
    all_gather x1, blocking collectives, head_shards(): lax.all_gather(lax.ppermute(w_out, both, there), 'fsdp', axis=0, tiled=True)  13.3 us
  transfers between devices with their start and end apart: 9, of which 5 were waited for; matrix products, arithmetic and copies ran while one was open for 13% of the time, Pallas kernels for 0%

profile of v2, /device:TPU:0, one launch (start us, length us, event | category | flops | bytes accessed | tf_op | source)
XLA Modules:
  0.0 344.7 jit_solution(4274570432147854965)
XLA Ops:
  8.0 1.1 copy.82
  9.1 1.0 copy.83
  10.1 1.0 copy.81
  11.1 5.4 %concatenate.43 = bf16[416]{0:T(512)(128)(2,1)S(1)} concatenate(bf16[32]{0:T(256)(128)(2,1)} %param.18, bf16[32]{0:T(256)(128)(2,1)} %param.19, bf16[32]{0:T(256)(128)(2,1)} %param.20, bf16[32]{0:T(256)(128)(2,1)} %param.21, bf16[32]{0:T(256)(128)(2,1)} %param.25, bf16[32]{0:T(256)(128)(2,1)} %param.29, bf16[96]{0:T(256)(128)(2,1)} %param.23, bf16[128]{0:T(256)(128)(2,1)} %param.27), dimensions={0} | concatenate | bytes 1664 | tf_op jit(solution)/shard_map/concatenate | solution.py:610
  16.9 33.5 %all_to_all.15 = bf16[8,32,1536]{2,1,0:T(8,128)(2,1)} all-to-all(bf16[8,32,1536]{2,1,0:T(8,128)(2,1)S(1)} %copy.61), channel_id=1, replica_groups=mesh['fsdp'=4,'ctx'=8] {'ctx'}, dimensions={0} | all-to-all | bytes 1572864 | tf_op jit(solution)/shard_map/all_to_all | solution.py:606
  52.2 13.3 %all_gather.14 = bf16[128,1024]{1,0:T(8,128)(2,1)S(1)} all-gather(bf16[32,1024]{1,0:T(8,128)(2,1)S(1)} %collective-permute-done), channel_id=1, replica_groups=mesh['fsdp'=4,'ctx'=8] {'fsdp'}, dimensions={0}, use_global_device_ids=true | all-gather | bytes 327680 | tf_op jit(solution)/shard_map/all_gather | solution.py:632
  65.5 5.0 %all-gather.9.cloned.1.call-done = bf16[1,1,1024,1024]{3,2,1,0:T(8,128)(2,1)} async-done(((bf16[1,1,128,1024]{3,2,1,0:T(8,128)(2,1)}), bf16[1,1,1024,1024]{3,2,1,0:T(8,128)(2,1)}) %all-gather.9.cloned.1.call-update) | async-done | bytes 2097168 | tf_op jit(solution)/shard_map/all_gather | solution.py:602
  70.5 2.1 convert_reduce_fusion
  73.4 26.4 %all-gather.5.cloned.1.call-done = bf16[1024,1536]{1,0:T(8,128)(2,1)} async-done(((bf16[256,1536]{1,0:T(8,128)(2,1)}), bf16[1024,1536]{1,0:T(8,128)(2,1)}) %all-gather.5.cloned.1.call-update) | async-done | bytes 3145744 | tf_op jit(solution)/shard_map/all_gather | solution.py:614
  99.8 1.7 slice.151
  101.5 1.8 reshape.325
  104.1 0.9 slice_convert_fusion.3
  105.2 2.5 convolution_add_fusion
  107.8 1.2 copy-done.5
  110.0 0.9 slice_bitcast_fusion.2
  111.9 1.7 fusion.104
  113.6 2.6 fusion.56
  116.3 1.9 fusion.3
  118.2 2.0 fusion
  120.2 5.2 %multiply_convert_fusion.1 = (bf16[1024,512]{1,0:T(8,128)(2,1)}, f32[1024,512]{1,0:T(8,128)}) fusion(f32[512]{0:T(512)S(1)} %dynamic-slice_convert_fusion, bf16[1024,1536]{1,0:T(8,128)(2,1)} %all-gather.5.cloned.1.call-done, bf16[1,1,1024,1024]{3,2,1,0:T(8,128)(2,1)S(1)} %copy-done.2, f32[1024]{0:T(1024)S(1)} %reshape.352, f32[1024]{0:T(1024)S(1)} %reshape.351, ...), kind=kOutput, calls=%fused_computation.38 | convolution fusion | flops 1083179008 | bytes 6309888 | tf_op jit(solution)/shard_map/dot_general | solution.py:669
  125.4 3.2 fusion.84
  128.6 30.3 %all-gather.7.cloned.1.call-done = bf16[1024,1024]{1,0:T(8,128)(2,1)} async-done(((bf16[128,1024]{1,0:T(8,128)(2,1)}), bf16[1024,1024]{1,0:T(8,128)(2,1)}) %all-gather.7.cloned.1.call-update) | async-done | bytes 2097168 | tf_op jit(solution)/shard_map/all_gather | solution.py:633
  158.9 2.4 convolution_convert_fusion.4
  161.5 5.9 %multiply_convert_fusion = bf16[2,1024,1024]{1,2,0:T(8,128)(2,1)S(1)} fusion(f32[2,1024,1024]{1,2,0:T(8,128)} %copy-done.1, f32[2,1024]{1,0:T(2,128)S(1)} %multiply_reduce_fusion, f32[2,1024]{1,0:T(2,128)S(1)} %log_add_fusion, pred[1024,1024]{0,1:T(8,128)(4,1)S(1)} %broadcast_compare_fusion, bf16[2,1024,64]{1,2,0:T(8,128)(2,1)S(1)} %bitcast.183, ...), kind=kOutput, calls=%fused_computation | convolution fusion | flops 283115520 | bytes 14172160 | tf_op jit(solution)/shard_map/hqd,hkd->hqk/dot_general | solution.py:565
  167.5 1.4 fusion.113
  170.0 2.5 fusion.18
  172.6 2.8 fusion.51
  175.5 4.5 %fusion.46 = f32[1024,1024]{1,0:T(8,128)} fusion(bf16[1024,1536]{1,0:T(8,128)(2,1)} %all-gather.5.cloned.1.call-done, f32[1024,128]{0,1:T(8,128)S(1)} %bitcast.180, f32[1024,128]{0,1:T(8,128)S(1)} %get-tuple-element.56, f32[1024,128]{0,1:T(8,128)S(1)} %get-tuple-element.55), kind=kOutput, calls=%fused_computation.74 | convolution fusion | flops 807665664 | bytes 6553600 | tf_op jit(solution)/shard_map/dot_general | solution.py:206
  180.2 4.0 %fusion.110 = (bf16[512]{0:T(512)(128)(2,1)S(1)}, bf16[1024,512]{1,0:T(8,128)(2,1)S(1)}) fusion(f32[1024,512]{1,0:T(8,128)} %get-tuple-element.65, f32[512]{0:T(512)S(1)} %dynamic-slice_convert_fusion, bf16[1024,1024]{1,0:T(8,128)(2,1)S(1)} %copy-done, bf16[1024,1536]{1,0:T(8,128)(2,1)} %all-gather.5.cloned.1.call-done), kind=kOutput, calls=%fused_computation.176 | convolution fusion | flops 1080032768 | bytes 6294528 | tf_op jit(solution)/shard_map/dot_general | solution.py:679
  184.2 5.1 %fusion.100 = (bf16[1024]{0:T(1024)(128)(2,1)S(1)}, bf16[1024]{0:T(1024)(128)(2,1)S(1)}, bf16[1024,1024]{1,0:T(8,128)(2,1)}, bf16[1024]{0:T(1024)(128)(2,1)S(1)}, bf16[1024]{0:T(1024)(128)(2,1)S(1)}) fusion(f32[1024]{0:T(1024)S(1)} %add_rsqrt_fusion, f32[1024]{0:T(1024)S(1)} %broadcast_multiply_fusion, bf16[1,1,1024,1024]{3,2,1,0:T(8,128)(2,1)S(1)} %copy-done.3, ...), kind=kOutput, calls=%fused_computation.166 | convolution fusion | flops 1087369216 | bytes 10510336 | tf_op jit(solution)/shard_map/dot_general | solution.py:206
  190.7 1.8 convert_element_type.236
  192.5 1.8 copy.67
  194.3 2.1 convolution_convert_fusion.3
  196.4 1.8 reshape.344
  198.1 1.8 copy.68
  199.9 4.0 %fusion.31 = bf16[1024,1664]{0,1:T(8,128)(2,1)} fusion(f32[1024,128]{0,1:T(8,128)} %bitcast.181, f32[1024,128]{0,1:T(8,128)S(1)} %get-tuple-element.56, f32[1024,128]{0,1:T(8,128)S(1)} %get-tuple-element.55, bf16[1,1,1024,1024]{3,2,1,0:T(8,128)(2,1)} %all-gather.9.cloned.1.call-done, f32[1024]{0:T(1024)S(1)} %reshape.355, f32[1024]{0:T(1024)S(1)} %reshape.354, ...), kind=kOutput, calls=%fused_computation.48 | convolution fusion | flops 814350336 | bytes 4472832 | tf_op jit(solution)/shard_map/dot_general | solution.py:200
  204.0 2.6 fusion.30
  206.6 2.3 fusion.29
  210.4 2.5 fusion.35
  213.0 2.1 add_convert_fusion.1
  215.0 3.6 %all-to-all-start.1 = ((bf16[8,128,1024]{2,1,0:T(8,128)(2,1)}), bf16[8,128,1024]{2,1,0:T(8,128)(2,1)S(1)}, u32[]{:S(2)}, u32[]{:S(2)}) async-start(bf16[8,128,1024]{2,1,0:T(8,128)(2,1)} %bitcast.174), calls=%async_computation.1 | async-start | bytes 4194304 | tf_op jit(solution)/shard_map/all_to_all | solution.py:672
  220.2 53.6 %all-to-all-done.1 = bf16[8,128,1024]{2,1,0:T(8,128)(2,1)S(1)} async-done(((bf16[8,128,1024]{2,1,0:T(8,128)(2,1)}), bf16[8,128,1024]{2,1,0:T(8,128)(2,1)S(1)}, u32[]{:S(2)}, u32[]{:S(2)}) %all-to-all-start.1) | async-done | bytes 2097184 | tf_op jit(solution)/shard_map/all_to_all | solution.py:672
  274.9 1.2 slice.225
  276.2 1.2 copy.69
  277.4 3.5 %all-to-all-start.2 = ((bf16[8,32,1536]{2,1,0:T(8,128)(2,1)}), bf16[8,32,1536]{2,1,0:T(8,128)(2,1)S(1)}, u32[]{:S(2)}, u32[]{:S(2)}) async-start(bf16[8,32,1536]{2,1,0:T(8,128)(2,1)} %bitcast.37), calls=%async_computation.4 | async-start | bytes 1572864 | tf_op jit(solution)/shard_map/all_to_all | solution.py:748
  281.2 47.0 %reduce-scatter.3.cloned.1.call-done = bf16[128,1024]{1,0:T(8,128)(2,1)} async-done(((bf16[1024,1024]{1,0:T(8,128)(2,1)}), bf16[128,1024]{1,0:T(8,128)(2,1)}) %reduce-scatter.3.cloned.1.call-update) | async-done | bytes 262160 | tf_op jit(solution)/shard_map/reduce_scatter | solution.py:702
  328.2 1.2 convert_reduce_fusion.2
  330.2 1.9 fusion.87
  (151 shorter events, 20.7 us)
Async XLA Ops:
  7.2 63.3 %all-gather.9.cloned.1.call-start = ((), (), s32[]{:S(2)}) async-start(), calls=%async_computation.9 | async-start | bytes 2359296 | tf_op jit(solution)/shard_map/all_gather | solution.py:602
  7.9 91.9 %all-gather.5.cloned.1.call-start = ((), (), s32[]{:S(2)}) async-start(), calls=%async_computation.5 | async-start | bytes 3932160 | tf_op jit(solution)/shard_map/all_gather | solution.py:614
  8.0 42.5 %copy-start.22 = (bf16[32,1024]{1,0:T(8,128)(2,1)S(1)}, bf16[32,1024]{1,0:T(8,128)(2,1)}, u32[]{:S(2)}) copy-start(bf16[32,1024]{1,0:T(8,128)(2,1)} %param.24) | copy-start | bytes 196612
  8.0 43.2 %copy-start.9 = (bf16[1,1,128,1024]{3,2,1,0:T(8,128)(2,1)S(1)}, bf16[1,1,128,1024]{3,2,1,0:T(8,128)(2,1)}, u32[]{:S(2)}) copy-start(bf16[1,1,128,1024]{3,2,1,0:T(8,128)(2,1)} %param.16) | copy-start | bytes 786436
  9.1 42.3 %copy-start.23 = (s32[8]{0:T(128)S(1)}, s32[8]{0:T(128)}, u32[]{:S(2)}) copy-start(s32[8]{0:T(128)} %param.17) | copy-start | bytes 100
  50.4 108.5 %all-gather.7.cloned.1.call-start = ((), (), s32[]{:S(2)}) async-start(), calls=%async_computation.6 | async-start | bytes 2359296 | tf_op jit(solution)/shard_map/all_gather | solution.py:633
  50.5 1.7 collective-permute-start
  70.5 2.2 copy-start.2
  107.7 1.2 copy-start.5
  109.7 165.3 %reduce-scatter.5.cloned.1.call-start = ((), (), s32[]{:S(2)}) async-start(), calls=%async_computation.8 | async-start | bytes 4259840 | tf_op jit(solution)/shard_map/reduce_scatter | solution.py:745
  110.0 3.5 %copy-start.6 = (f32[1024,384]{0,1:T(8,128)S(1)}, f32[1024,384]{0,1:T(8,128)}, u32[]{:S(2)}) copy-start(f32[1024,384]{0,1:T(8,128)} %copy-done.5) | copy-start | bytes 4718596
  116.2 1.9 copy-start.11
  116.2 1.9 copy-start.16
  118.2 7.2 %copy-start.1 = (f32[2,1024,1024]{1,2,0:T(8,128)}, f32[2,1024,1024]{1,2,0:T(8,128)S(1)}, u32[]{:S(2)}) copy-start(f32[2,1024,1024]{1,2,0:T(8,128)S(1)} %get-tuple-element.67) | copy-start | bytes 25165828
  120.2 5.2 %copy-start.19 = (bf16[1024,128]{0,1:T(8,128)(2,1)S(1)}, bf16[1024,128]{0,1:T(8,128)(2,1)}, u32[]{:S(2)}) copy-start(bf16[1024,128]{0,1:T(8,128)(2,1)} %slice.261) | copy-start | bytes 786436
  128.6 32.9 %copy-start.20 = (bf16[1024,128]{0,1:T(8,128)(2,1)S(1)}, bf16[1024,128]{0,1:T(8,128)(2,1)}, u32[]{:S(2)}) copy-start(bf16[1024,128]{0,1:T(8,128)(2,1)} %slice.261) | copy-start | bytes 786436
  161.3 8.6 %slice-start = ((s8[8388608]{0:T(1024)(128)(4,1)}), s8[4194304]{0:T(1024)(128)(4,1)S(1)}, s32[]{:S(2)}) async-start(s8[8388608]{0:T(1024)(128)(4,1)} %bitcast.172), calls=%async_computation.10 | async-start | bytes 8388608
  161.5 6.0 %copy-start.17 = (bf16[1024,128]{0,1:T(8,128)(2,1)S(1)}, bf16[1024,128]{0,1:T(8,128)(2,1)}, u32[]{:S(2)}) copy-start(bf16[1024,128]{0,1:T(8,128)(2,1)} %copy-done.16) | copy-start | bytes 786436
  161.5 8.5 %slice-start.1 = ((s8[8388608]{0:T(1024)(128)(4,1)}), s8[4194304]{0:T(1024)(128)(4,1)S(1)}, s32[]{:S(2)}) async-start(s8[8388608]{0:T(1024)(128)(4,1)} %bitcast.172), calls=%async_computation.11 | async-start | bytes 8388608
  167.5 1.5 copy-start.12
  172.5 2.9 copy-start.13
  175.5 4.7 %copy-start = (bf16[1024,1024]{1,0:T(8,128)(2,1)S(1)}, bf16[1024,1024]{1,0:T(8,128)(2,1)}, u32[]{:S(2)}) copy-start(bf16[1024,1024]{1,0:T(8,128)(2,1)} %all-gather.7.cloned.1.call-done) | copy-start | bytes 6291460
  180.2 4.0 %copy-start.3 = (bf16[1,1,1024,1024]{3,2,1,0:T(8,128)(2,1)S(1)}, bf16[1,1,1024,1024]{3,2,1,0:T(8,128)(2,1)}, u32[]{:S(2)}) copy-start(bf16[1,1,1024,1024]{3,2,1,0:T(8,128)(2,1)} %all-gather.9.cloned.1.call-done) | copy-start | bytes 6291460
  180.2 4.0 %copy-start.8 = (f32[1024,1024]{1,0:T(8,128)S(1)}, f32[1024,1024]{1,0:T(8,128)}, u32[]{:S(2)}) copy-start(f32[1024,1024]{1,0:T(8,128)} %fusion.46) | copy-start | bytes 12582916
  184.2 5.2 %copy-start.26 = (bf16[1024,512]{1,0:T(8,128)(2,1)}, bf16[1024,512]{1,0:T(8,128)(2,1)S(1)}, u32[]{:S(2)}) copy-start(bf16[1024,512]{1,0:T(8,128)(2,1)S(1)} %get-tuple-element.71) | copy-start | bytes 3145732
  199.9 4.0 %copy-start.4 = (bf16[1,1,1024,1024]{3,2,1,0:T(8,128)(2,1)S(1)}, bf16[1,1,1024,1024]{3,2,1,0:T(8,128)(2,1)}, u32[]{:S(2)}) copy-start(bf16[1,1,1024,1024]{3,2,1,0:T(8,128)(2,1)} %all-gather.9.cloned.1.call-done) | copy-start | bytes 6291460
  199.9 4.0 %copy-start.27 = (bf16[1024,512]{1,0:T(8,128)(2,1)S(1)}, bf16[1024,512]{1,0:T(8,128)(2,1)}, u32[]{:S(2)}) copy-start(bf16[1024,512]{1,0:T(8,128)(2,1)} %copy-done.26) | copy-start | bytes 3145732
  204.0 2.6 copy-start.24
  206.6 2.3 copy-start.14
  206.6 3.0 copy-start.15
  208.9 1.5 copy-start.25
  210.4 2.6 copy-start.18
  215.0 58.7 %all-to-all-start.1 = ((bf16[8,128,1024]{2,1,0:T(8,128)(2,1)}), bf16[8,128,1024]{2,1,0:T(8,128)(2,1)S(1)}, u32[]{:S(2)}, u32[]{:S(2)}) async-start(bf16[8,128,1024]{2,1,0:T(8,128)(2,1)} %bitcast.174), calls=%async_computation.1 | async-start | bytes 4194304 | tf_op jit(solution)/shard_map/all_to_all | solution.py:672
  218.7 55.4 %copy-start.7 = (bf16[1,1,128,1024]{3,2,1,0:T(8,128)(2,1)S(1)}, bf16[1,1,128,1024]{3,2,1,0:T(8,128)(2,1)}, u32[]{:S(2)}) copy-start(bf16[1,1,128,1024]{3,2,1,0:T(8,128)(2,1)} %param.15) | copy-start | bytes 786436
  218.7 109.5 %reduce-scatter.3.cloned.1.call-start = ((), (), s32[]{:S(2)}) async-start(), calls=%async_computation.7 | async-start | bytes 2359296 | tf_op jit(solution)/shard_map/reduce_scatter | solution.py:702
  274.1 56.1 %copy-start.10 = (bf16[1,1,128,1024]{3,2,1,0:T(8,128)(2,1)S(1)}, bf16[1,1,128,1024]{3,2,1,0:T(8,128)(2,1)}, u32[]{:S(2)}) copy-start(bf16[1,1,128,1024]{3,2,1,0:T(8,128)(2,1)} %param.16) | copy-start | bytes 786436
  274.9 54.4 %slice-start.2 = ((bf16[256,1664]{0,1:T(8,128)(2,1)}), bf16[256,128]{0,1:T(8,128)(2,1)S(1)}, s32[]{:S(2)}) async-start(bf16[256,1664]{0,1:T(8,128)(2,1)} %reduce-scatter.5.cloned.1.call-done), calls=%async_computation.12 | async-start | bytes 131072 | tf_op jit(solution)/shard_map/slice | solution.py:747
  277.4 55.5 %all-to-all-start.2 = ((bf16[8,32,1536]{2,1,0:T(8,128)(2,1)}), bf16[8,32,1536]{2,1,0:T(8,128)(2,1)S(1)}, u32[]{:S(2)}, u32[]{:S(2)}) async-start(bf16[8,32,1536]{2,1,0:T(8,128)(2,1)} %bitcast.37), calls=%async_computation.4 | async-start | bytes 1572864 | tf_op jit(solution)/shard_map/all_to_all | solution.py:748
  329.6 2.6 collective-permute-start.1
  333.8 4.3 %copy-start.21 = (f32[32]{0:T(128)}, f32[32]{0:T(128)S(1)}, u32[]{:S(2)}) copy-start(f32[32]{0:T(128)S(1)} %get-tuple-element.105) | copy-start | bytes 388
Sparse Core Ops, SparseCore 0:
  10.1 60.3 all-gather.8
  72.1 27.7 all-gather.4
  109.8 49.0 all-gather.6
  210.5 37.9 reduce-scatter.4
  251.9 76.2 reduce-scatter.2
